TPU v7x, 128 devices: a whole 4x4x4 slice. The times are simulated.
128 devices in a mesh: ty: 8 (over x_lo, z), tx: 4 (over x_hi, core), pat: 4 (over y).
Axes of the slice: x: 4 (x_hi: 2, x_lo: 2; x = x_hi * 2 + x_lo), y: 4, z: 4, core: 2. Of those that a mesh axis runs over, the one named last changes fastest.
Arguments:
- estimate: float32 [32, 128, 1024], P(None, 'ty', 'tx'), may hold values from 0.5 to 1.5, as said below
- data: float32 [8, 32, 128, 1024], P('pat', None, 'ty', 'tx'), may hold values from 0.1 to 6, as said below
- axial: float32 [32, 32], replicated, may hold values from 0 to 0.6, as said below
- lateral_kernel: float32 [9, 9], replicated, may hold values from 0.01 to 0.04
- psf_radius: int32 [9], replicated, may hold values from 0 to 4
- pattern_codes: int32 [2, 8], replicated, may hold values from 0 to 4, as said below
Outputs:
- object_out: float32 [32, 128, 1024], P(None, 'ty', 'tx')
- residual_rms: float32 [4], replicated
Inputs may be any that keep to these rules, and one draw needn't show every extreme that they name: `estimate`: positive values. `data`: positive photon counts. `axial`: nonnegative entries. `pattern_codes`: angle indices are 0 to 2, phase indices 0 to 4.
All inputs are finite; a program needn't handle non-finite values.
Results may differ from a plain program's by a relative error of at most 0.0003.
The roundings to bfloat16 on the way count: a program that leaves them out, or rounds other values in their place, can miss the bound.
Values may be sent and summed in bfloat16 or wider, within the bound.
A program may use at most 128 MiB of HBM per device.

v0:
```python
import functools
import math

import jax
import jax.numpy as jnp
from jax import lax
from jax.experimental import pallas as pl
from jax.experimental.pallas import tpu as pltpu
from jax.sharding import PartitionSpec as P

ITERS = 4
TAPS = 9
NPAT = 8
LANES = 128
COSINES = [math.cos(2.0 * math.pi * m / 5.0) for m in range(5)]
MESH = pl.DeviceIdType.MESH


def lane_iota(shape):
    return lax.broadcasted_iota(jnp.int32, shape, len(shape) - 1)


def row_iota(shape):
    return lax.broadcasted_iota(jnp.int32, shape, len(shape) - 2)


def block_transpose(tiles):
    group = lane_iota(tiles[0].shape) // 16
    tiles = list(tiles)
    for bit in (4, 2, 1):
        keep = (group & bit) == 0
        for k in range(8):
            if k & bit:
                continue
            low, high = tiles[k], tiles[k + bit]
            axis = low.ndim - 1
            tiles[k] = jnp.where(keep, low, pltpu.roll(high, 16 * bit, axis))
            tiles[k + bit] = jnp.where(keep, pltpu.roll(low, LANES - 16 * bit, axis), high)
    return tiles


def kernel(
    full_rows,
    full_cols,
    est_ref,
    data_ref,
    axial_ref,
    taps_ref,
    radius_ref,
    codes_ref,
    out_ref,
    squares_ref,
    grid_ref,
    final_ref,
    home_ref,
    data_tiles,
    top_ref,
    bottom_ref,
    left_ref,
    right_ref,
    lit_ref,
    blur_ref,
    pred_ref,
    quot_ref,
    forward_ref,
    adjoint_ref,
    axial_fwd,
    axial_adj,
    wave_ext,
    wave_in,
    planes_ref,
    mask_ext,
    valid_ref,
    norm_ref,
    halo_send,
    halo_recv,
    row_send,
    row_recv,
    edge_send,
    left_recv,
    right_recv,
    pat_send,
    pat_recv,
    out_send,
    out_recv,
):
    ty, tx, q = lax.axis_index("ty"), lax.axis_index("tx"), lax.axis_index("pat")
    nty, ntx, npat = lax.axis_size("ty"), lax.axis_size("tx"), lax.axis_size("pat")
    ncol = ntx * npat
    column = tx * npat + q

    def at(dty, dcol):
        c = lax.rem(column + dcol + ncol, ncol)
        return {"ty": lax.rem(ty + dty + nty, nty), "tx": c // npat, "pat": lax.rem(c, npat)}

    def peer(d):
        return {"ty": ty, "tx": tx, "pat": lax.rem(q + d, npat)}

    barrier = pltpu.get_barrier_semaphore()
    greeted = 0
    for dty in (-1, 0, 1):
        for dtx in (-1, 0, 1):
            for dq in range(npat):
                if dty == 0 and dtx == 0 and dq == 0:
                    continue
                pl.semaphore_signal(
                    barrier,
                    inc=1,
                    device_id={
                        "ty": lax.rem(ty + dty + nty, nty),
                        "tx": lax.rem(tx + dtx + ntx, ntx),
                        "pat": lax.rem(q + dq, npat),
                    },
                    device_id_type=MESH,
                )
                greeted += 1

    for strip in range(2):
        for half in range(2):
            rows = [est_ref[8 * strip + y, :, LANES * half : LANES * (half + 1)] for y in range(8)]
            for k, tile in enumerate(block_transpose(rows)):
                final_ref[2 * half + k // 4, k % 4, strip] = tile
    grid_ref[0, 1:5, 1:3] = final_ref[q]

    pl.semaphore_wait(barrier, greeted)

    def halo_copies(t):
        moves = [
            ((slice(1, 5), 1), (slice(1, 5), 3), -1, 0),
            ((slice(1, 5), 2), (slice(1, 5), 0), 1, 0),
            ((1, slice(1, 3)), (5, slice(1, 3)), 0, -1),
            ((4, slice(1, 3)), (0, slice(1, 3)), 0, 1),
            ((1, 1), (5, 3), -1, -1),
            ((4, 1), (0, 3), -1, 1),
            ((1, 2), (5, 0), 1, -1),
            ((4, 2), (0, 0), 1, 1),
        ]
        copies = []
        for k, (source, target, dty, dcol) in enumerate(moves):
            copies.append(
                pltpu.make_async_remote_copy(
                    src_ref=grid_ref.at[(t, *source)],
                    dst_ref=grid_ref.at[(t, *target)],
                    send_sem=halo_send.at[t, k],
                    recv_sem=halo_recv.at[t, k],
                    device_id=at(dty, dcol),
                    device_id_type=MESH,
                )
            )
        return copies

    for copy in halo_copies(0):
        copy.start()

    row_copies = [
        pltpu.make_async_remote_copy(
            src_ref=data_ref.at[12:16],
            dst_ref=top_ref,
            send_sem=row_send.at[0],
            recv_sem=row_recv.at[0],
            device_id=at(1, 0),
            device_id_type=MESH,
        ),
        pltpu.make_async_remote_copy(
            src_ref=data_ref.at[0:4],
            dst_ref=bottom_ref,
            send_sem=row_send.at[1],
            recv_sem=row_recv.at[1],
            device_id=at(-1, 0),
            device_id_type=MESH,
        ),
    ]
    for copy in row_copies:
        copy.start()

    def data_row(row, block, half):
        rows = slice(8 * block, 8 * block + 8)
        lanes = slice(LANES * half, LANES * (half + 1))
        if row < 4:
            return top_ref[row, rows, lanes]
        if row < 20:
            return data_ref[row - 4, rows, lanes]
        return bottom_ref[row - 20, rows, lanes]

    def make_strip(strip):
        first = lane_iota((8, LANES)) < 4
        for block in range(8):
            at_rows = slice(8 * block, 8 * block + 8)
            low = [pltpu.roll(data_row(8 * strip + y, block, 0), 4, 1) for y in range(8)]
            high = [pltpu.roll(data_row(8 * strip + y, block, 1), 4, 1) for y in range(8)]
            for k, tile in enumerate(block_transpose(low)):
                home_ref[k, strip, at_rows] = tile
            mixed = [jnp.where(first, a, b) for a, b in zip(low, high)]
            for k, tile in enumerate(block_transpose(mixed)):
                home_ref[8 + k, strip, at_rows] = tile
            last = high[0]
            group = lane_iota((8, LANES)) // 16
            for y in range(1, 8):
                last = jnp.where(group == y, pltpu.roll(high[y], 16 * y, 1), last)
            home_ref[16, strip, at_rows] = last

    def strip_copies(strip):
        copies = []
        for d in range(1, npat):
            to = lax.rem(q + d, npat)
            copies.append(
                pltpu.make_async_remote_copy(
                    src_ref=home_ref.at[pl.ds(4 * to, 5), strip],
                    dst_ref=data_tiles.at[q, :, strip],
                    send_sem=pat_send.at[strip, d - 1],
                    recv_sem=pat_recv.at[strip, d - 1],
                    device_id=peer(d),
                    device_id_type=MESH,
                )
            )
        return copies

    def edge_copies():
        return [
            pltpu.make_async_remote_copy(
                src_ref=home_ref.at[16],
                dst_ref=left_ref.at[q],
                send_sem=edge_send.at[0],
                recv_sem=left_recv.at[q],
                device_id={"ty": ty, "tx": lax.rem(tx + 1, ntx), "pat": 0},
                device_id_type=MESH,
            ),
            pltpu.make_async_remote_copy(
                src_ref=home_ref.at[0],
                dst_ref=right_ref.at[q],
                send_sem=edge_send.at[1],
                recv_sem=right_recv.at[q],
                device_id={"ty": ty, "tx": lax.rem(tx + ntx - 1, ntx), "pat": npat - 1},
                device_id_type=MESH,
            ),
        ]

    make_strip(1)
    for copy in strip_copies(1):
        copy.start()

    lane = lane_iota((LANES, LANES))
    line = row_iota((LANES, LANES))
    for backward in (False, True):
        target = adjoint_ref if backward else forward_ref
        target[...] = jnp.zeros_like(target)
        for block in range(2):
            row_gap = 8 * block + line // 16 - lane // 16
            for step in range(2):
                col_gap = 16 * step + lax.rem(line, 16) - lax.rem(lane, 16)
                total = jnp.zeros((LANES, LANES), jnp.float32)
                for i in range(TAPS):
                    here = jnp.zeros((LANES, LANES), jnp.float32)
                    for j in range(TAPS):
                        ki, kj = (TAPS - 1 - i, TAPS - 1 - j) if backward else (i, j)
                        tap = jnp.where(abs(kj - 4) <= radius_ref[ki], taps_ref[ki, kj], 0.0)
                        here = jnp.where(col_gap == j, tap, here)
                    total = jnp.where(row_gap == i, here, total)
                values = total.astype(jnp.bfloat16)
                for out_chunk in range(2):
                    start = 256 * (out_chunk + step) + LANES * block
                    target[start : start + LANES, LANES * out_chunk : LANES * (out_chunk + 1)] = values

    spread = (row_iota((256, 32)) % 32 == lane_iota((256, 32))).astype(jnp.bfloat16)
    axial_b = axial_ref[...].astype(jnp.bfloat16)
    same = row_iota((256, 256)) // 32 == lane_iota((256, 256)) // 32
    nt = (((1,), (1,)), ((), ()))
    right_fwd = lax.dot_general(axial_b, spread, nt, preferred_element_type=jnp.float32)
    full = jnp.dot(spread, right_fwd.astype(jnp.bfloat16), preferred_element_type=jnp.float32)
    axial_fwd[...] = jnp.where(same, full, 0.0).astype(jnp.bfloat16)
    left_adj = lax.dot_general(spread, axial_b, nt, preferred_element_type=jnp.float32)
    full = lax.dot_general(left_adj.astype(jnp.bfloat16), spread, nt, preferred_element_type=jnp.float32)
    axial_adj[...] = jnp.where(same, full, 0.0).astype(jnp.bfloat16)

    plane = row_iota((32, LANES)).astype(jnp.float32)
    planes_ref[...] = jnp.cos(plane * (2.0 * math.pi * 3.0 / 32.0))

    def positions(tile, strips, offset):
        spot = lane_iota(tile.shape)
        chunk, strip = tile // strips, tile % strips
        y = ty * 16 + 8 * strip - offset + spot // 16
        x = column * 64 + 16 * chunk - offset + spot % 16
        return y, x

    def waves(count, strips, offset):
        shape = (count * NPAT, LANES)
        index = row_iota(shape)
        y, x = positions(index // NPAT, strips, offset)
        pattern = index % NPAT
        angle = jnp.zeros(shape, jnp.int32)
        phase = jnp.zeros(shape, jnp.int32)
        for p in range(NPAT):
            angle = jnp.where(pattern == p, codes_ref[0, p], angle)
            phase = jnp.where(pattern == p, codes_ref[1, p], phase)
        cx = jnp.where(angle == 0, 2, -1)
        cy = jnp.where(angle == 0, 0, jnp.where(angle == 1, 2, -2))
        value = cx * x + cy * y + phase
        wide = value.astype(jnp.float32)
        m = wide - 5.0 * jnp.floor((wide + 0.5) * 0.2)
        wave = jnp.full(shape, COSINES[0], jnp.float32)
        for k in range(1, 5):
            wave = jnp.where(m == float(k), COSINES[k], wave)
        return 0.7 * wave

    wave_ext[...] = waves(20, 4, 8)
    wave_in[...] = waves(8, 2, 0)

    def inside(shape, strips, offset):
        y, x = positions(row_iota(shape), strips, offset)
        return (y >= 0) & (y < full_rows) & (x >= 0) & (x < full_cols)

    mask_ext[...] = inside((24, LANES), 4, 8).astype(jnp.float32)
    tile15 = (16, LANES)
    valid = inside(tile15, 3, 4) & ((row_iota(tile15) < 12) | (lane_iota(tile15) % 16 < 8))
    valid_ref[...] = valid.astype(jnp.float32)

    for copy in row_copies:
        copy.wait_recv()
    make_strip(0)
    make_strip(2)
    for copy in strip_copies(0) + strip_copies(2) + edge_copies():
        copy.start()
    data_tiles[q] = home_ref[pl.ds(4 * q, 5)]

    column_sum = lax.dot_general(
        axial_b, jnp.ones((32, LANES), jnp.bfloat16), (((0,), (0,)), ((), ())),
        preferred_element_type=jnp.float32,
    )
    cover_in = [
        jnp.broadcast_to(valid_ref[k : k + 1, :], (16, LANES)).astype(jnp.bfloat16)
        for k in range(15)
    ]
    plane_wave = planes_ref[...]
    for strip in range(2):
        for chunk in (0, 2):
            window = jnp.concatenate(
                [cover_in[3 * (chunk + k) + strip + a] for k in range(3) for a in range(2)], axis=1
            )
            cover = jnp.dot(window, adjoint_ref[...], preferred_element_type=jnp.float32)
            cover = cover.astype(jnp.bfloat16).astype(jnp.float32)
            for k in range(2):
                tile = 2 * (chunk + k) + strip
                row = cover[0:1, LANES * k : LANES * (k + 1)]
                light = jnp.zeros((32, LANES), jnp.float32)
                for p in range(NPAT):
                    light = light + (1.0 + wave_in[NPAT * tile + p : NPAT * tile + p + 1, :] * plane_wave)
                norm_ref[tile] = light * (row * column_sum)

    own = lane_iota((8, LANES))
    own_col, own_row = own % 16, own // 16

    def inner_mask(tile):
        chunk, strip = tile // 3, tile % 3
        x, y = 16 * chunk + own_col, 8 * strip + own_row
        return (x >= 4) & (x < 68) & (y >= 4) & (y < 20)

    def predict(strip, chunk):
        tile = 4 * chunk + strip
        if chunk == 4:
            return jnp.dot(
                blur_ref[:, LANES * tile : LANES * (tile + 2)],
                forward_ref[0:256, 0:LANES],
                preferred_element_type=jnp.float32,
            )
        window = jnp.concatenate(
            [blur_ref[:, LANES * (tile + 4 * k) : LANES * (tile + 4 * k + 2)] for k in range(3)], axis=1
        )
        return jnp.dot(window, forward_ref[...], preferred_element_type=jnp.float32)

    def compare(strip, chunk, predicted, squares):
        for k in range(predicted.shape[1] // LANES):
            tile = 3 * (chunk + k) + strip
            ok = valid_ref[tile : tile + 1, :]
            filler = 1.0 - ok
            total = jnp.zeros((8, LANES), jnp.float32)
            for source in range(4):
                data = data_tiles[source, chunk + k, strip]
                guess = predicted[64 * source : 64 * (source + 1), LANES * k : LANES * (k + 1)]
                misfit = data - guess
                total = total + jnp.sum((misfit * misfit).reshape(8, 8, LANES), axis=0)
                quotient = (data * ok) / (guess + filler)
                quot_ref[64 * source : 64 * (source + 1), LANES * tile : LANES * (tile + 1)] = (
                    quotient.astype(jnp.bfloat16)
                )
            squares = squares + jnp.where(inner_mask(tile), total, 0.0)
        return squares

    def iteration(t, first):
        copies = halo_copies(t)
        for copy in copies:
            copy.wait_recv()
        wave_z = planes_ref[...]
        left_half = lane_iota((32, LANES)) % 16 < 8
        for chunk in range(5):
            for strip in range(4):
                tile = 4 * chunk + strip
                a, b = grid_ref[t, chunk, strip], grid_ref[t, chunk + 1, strip]
                value = jnp.where(left_half, pltpu.roll(a, LANES - 8, 1), pltpu.roll(b, 8, 1))
                value = value * mask_ext[tile : tile + 1, :]
                for p in range(NPAT):
                    light = 1.0 + wave_ext[NPAT * tile + p : NPAT * tile + p + 1, :] * wave_z
                    lit_ref[32 * p : 32 * (p + 1), LANES * tile : LANES * (tile + 1)] = (
                        light * value
                    ).astype(jnp.bfloat16)
        for pair in range(10):
            lanes = slice(256 * pair, 256 * (pair + 1))
            blur_ref[:, lanes] = jnp.dot(
                axial_fwd[...], lit_ref[:, lanes], preferred_element_type=jnp.float32
            ).astype(jnp.bfloat16)
        squares = jnp.zeros((8, LANES), jnp.float32)
        order = [(strip, chunk) for strip in range(3) for chunk in (0, 2, 4)]
        if first:
            for strip, chunk in order:
                width = LANES if chunk == 4 else 2 * LANES
                tile = 5 * strip + chunk
                pred_ref[:, LANES * tile : LANES * tile + width] = predict(strip, chunk)
            for strip in range(3):
                for copy in strip_copies(strip):
                    copy.wait_recv()

            @pl.when(q == 0)
            def _():
                for source in range(4):
                    edge_in(left_ref.at[source], left_recv.at[source])
                    keep = lane_iota((64, LANES)) % 16 < 4
                    for strip in range(3):
                        data_tiles[source, 0, strip] = jnp.where(
                            keep, left_ref[source, strip], data_tiles[source, 0, strip]
                        )

            @pl.when(q == npat - 1)
            def _():
                for source in range(4):
                    edge_in(right_ref.at[source], right_recv.at[source])
                    keep = lane_iota((64, LANES)) % 16 < 4
                    for strip in range(3):
                        data_tiles[source, 4, strip] = jnp.where(
                            keep, data_tiles[source, 4, strip], right_ref[source, strip]
                        )

            for strip, chunk in order:
                width = LANES if chunk == 4 else 2 * LANES
                tile = 5 * strip + chunk
                squares = compare(
                    strip, chunk, pred_ref[:, LANES * tile : LANES * tile + width], squares
                )
        else:
            for strip, chunk in order:
                squares = compare(strip, chunk, predict(strip, chunk), squares)
        squares_ref[t] = squares
        updated = []
        for strip in range(2):
            for chunk in (0, 2):
                tile = 3 * chunk + strip
                window = jnp.concatenate(
                    [quot_ref[:, LANES * (tile + 3 * k) : LANES * (tile + 3 * k + 2)] for k in range(3)],
                    axis=1,
                )
                spread_back = jnp.dot(
                    window, adjoint_ref[...], preferred_element_type=jnp.float32
                ).astype(jnp.bfloat16)
                gathered = jnp.dot(
                    axial_adj[...], spread_back, preferred_element_type=jnp.float32
                )
                for k in range(2):
                    here = 2 * (chunk + k) + strip
                    summed = jnp.zeros((32, LANES), jnp.float32)
                    for p in range(NPAT):
                        light = 1.0 + wave_in[NPAT * here + p : NPAT * here + p + 1, :] * wave_z
                        summed = summed + light * gathered[
                            32 * p : 32 * (p + 1), LANES * k : LANES * (k + 1)
                        ]
                    current = grid_ref[t, 1 + chunk + k, 1 + strip]
                    updated.append((chunk + k, strip, current * summed / norm_ref[here]))
        return updated, copies

    def edge_in(ref, sem):
        pltpu.make_async_copy(ref, ref, sem).wait()

    def advance(t, first):
        updated, copies = iteration(t, first)
        for chunk, strip, value in updated:
            grid_ref[t + 1, 1 + chunk, 1 + strip] = value
        for copy in halo_copies(t + 1):
            copy.start()
        for copy in copies:
            copy.wait_send()

    advance(0, True)
    for copy in row_copies + strip_copies(0) + strip_copies(1) + strip_copies(2) + edge_copies():
        copy.wait_send()

    @pl.loop(1, ITERS - 1)
    def _(t):
        advance(t, False)

    updated, copies = iteration(ITERS - 1, False)
    for chunk, strip, value in updated:
        final_ref[q, chunk, strip] = value
    outs = [
        pltpu.make_async_remote_copy(
            src_ref=final_ref.at[q],
            dst_ref=final_ref.at[q],
            send_sem=out_send.at[d - 1],
            recv_sem=out_recv.at[d - 1],
            device_id=peer(d),
            device_id_type=MESH,
        )
        for d in range(1, npat)
    ]
    for copy in outs:
        copy.start()
    for copy in copies:
        copy.wait_send()
    for copy in outs:
        copy.wait()
    for strip in range(2):
        for half in range(2):
            tiles = [final_ref[2 * half + k // 4, k % 4, strip] for k in range(8)]
            for y, row in enumerate(block_transpose(tiles)):
                out_ref[8 * strip + y, :, LANES * half : LANES * (half + 1)] = row


def per_device(estimate, data, axial, lateral_kernel, psf_radius, pattern_codes):
    planes, height, width = estimate.shape
    local = data.shape[0]
    full_rows = height * lax.axis_size("ty")
    full_cols = width * lax.axis_size("tx")
    est_rows = estimate.transpose(1, 0, 2)
    data_rows = data.transpose(2, 0, 1, 3).reshape(height, local * planes, width)
    vmem = pl.BlockSpec(memory_space=pltpu.VMEM)
    smem = pl.BlockSpec(memory_space=pltpu.SMEM)
    f32, bf16 = jnp.float32, jnp.bfloat16
    dma = pltpu.SemaphoreType.DMA
    rows, squares = pl.pallas_call(
        functools.partial(kernel, full_rows, full_cols),
        name="deconvolve",
        out_shape=(
            jax.ShapeDtypeStruct((height, planes, width), f32),
            jax.ShapeDtypeStruct((ITERS, 8, LANES), f32),
        ),
        in_specs=[vmem, vmem, vmem, smem, smem, smem],
        out_specs=(vmem, vmem),
        scratch_shapes=[
            pltpu.VMEM((ITERS, 6, 4, 32, LANES), f32),
            pltpu.VMEM((4, 4, 2, 32, LANES), f32),
            pltpu.VMEM((17, 3, 64, LANES), f32),
            pltpu.VMEM((4, 5, 3, 64, LANES), f32),
            pltpu.VMEM((4, 64, 256), f32),
            pltpu.VMEM((4, 64, 256), f32),
            pltpu.VMEM((4, 3, 64, LANES), f32),
            pltpu.VMEM((4, 3, 64, LANES), f32),
            pltpu.VMEM((256, 20 * LANES), bf16),
            pltpu.VMEM((256, 20 * LANES), bf16),
            pltpu.VMEM((256, 15 * LANES), f32),
            pltpu.VMEM((256, 15 * LANES), bf16),
            pltpu.VMEM((768, 256), bf16),
            pltpu.VMEM((768, 256), bf16),
            pltpu.VMEM((256, 256), bf16),
            pltpu.VMEM((256, 256), bf16),
            pltpu.VMEM((20 * NPAT, LANES), f32),
            pltpu.VMEM((8 * NPAT, LANES), f32),
            pltpu.VMEM((32, LANES), f32),
            pltpu.VMEM((24, LANES), f32),
            pltpu.VMEM((16, LANES), f32),
            pltpu.VMEM((8, 32, LANES), f32),
            dma((ITERS, 8)),
            dma((ITERS, 8)),
            dma((2,)),
            dma((2,)),
            dma((2,)),
            dma((4,)),
            dma((4,)),
            dma((3, 3)),
            dma((3, 3)),
            dma((3,)),
            dma((3,)),
        ],
        compiler_params=pltpu.CompilerParams(
            collective_id=0, has_side_effects=True, vmem_limit_bytes=56 * 1024 * 1024
        ),
    )(est_rows, data_rows, axial, lateral_kernel, psf_radius, pattern_codes)
    total = lax.psum(jnp.sum(squares, axis=(1, 2)), ("ty", "tx", "pat"))
    cells = float(local * lax.axis_size("pat") * planes * full_rows * full_cols)
    return rows.transpose(1, 0, 2), jnp.sqrt(total / cells)


def solution(mesh):
    in_specs = (P(None, "ty", "tx"), P("pat", None, "ty", "tx"), P(), P(), P(), P())
    out_specs = (P(None, "ty", "tx"), P())
    return jax.shard_map(
        per_device, mesh=mesh, in_specs=in_specs, out_specs=out_specs, check_vma=False
    )
```

profile of v0, /device:TPU:1, one launch (start us, length us, event | category | flops | bytes accessed | tf_op | source)
XLA Modules:
  0.0 155.0 jit_solution(1923878290422654314)
XLA Ops:
  0.6 0.0 copy-start
  0.6 2.2 %copy.12 = f32[32,16,256]{2,0,1:T(8,128)} copy(f32[32,16,256]{2,1,0:T(8,128)} %param.6) | data formatting | bytes 1048576 | tf_op args[0]
  2.9 0.0 copy-done
  2.9 1.6 %copy.9 = f32[16,2,32,256]{3,2,1,0:T(8,128)} copy(f32[16,2,32,256]{3,0,2,1:T(8,128)S(1)} %bitcast.8) | data formatting | bytes 2097152 | tf_op jit(solution)/shard_map/transpose | solution.py:530
  4.5 83.5 %deconvolve.1 = (f32[16,32,256]{2,1,0:T(8,128)}, f32[4,8,128]{2,1,0:T(8,128)}) custom-call(f32[16,32,256]{2,1,0:T(8,128)} %bitcast.7, f32[16,64,256]{2,1,0:T(8,128)} %bitcast.6, f32[32,32]{1,0:T(8,128)} %axial_ref.1, f32[9,9]{1,0:T(8,128)} %taps_ref.1, s32[9]{0:T(128)} %radius_ref.1, s32[2,8]{1,0:T(2,128)} %codes_ref.1), custom_call_target="tpu_custom_call" | custom-call | tf_op jit(solution)/shard_map/deconvolve/pallas_call | solution.py:535
  87.9 0.0 copy-start.1
  88.0 2.1 %copy.10 = f32[32,16,256]{2,1,0:T(8,128)} copy(f32[32,16,256]{2,0,1:T(8,128)} %bitcast.9) | data formatting | bytes 1048576
  90.1 0.0 copy-done.1
  90.1 0.1 reduce_sum.9
  90.2 64.2 %psum.7 = f32[4]{0:T(128)S(1)} all-reduce(f32[4]{0:T(128)S(1)} %reduce_sum.9), channel_id=1, replica_groups=mesh['ty'=8,'tx'=4,'pat'=4] {'ty','tx','pat'}, use_global_device_ids=true, to_apply=%region_1.0 | all-reduce | flops 4 | bytes 32 | tf_op jit(solution)/shard_map/psum | solution.py:583
  154.5 0.5 multiply_sqrt_fusion
Async XLA Ops:
  0.6 2.2 %copy-start = (f32[2,32,16,256]{3,2,1,0:T(8,128)S(1)}, f32[2,32,16,256]{3,2,1,0:T(8,128)}, u32[]{:S(2)}) copy-start(f32[2,32,16,256]{3,2,1,0:T(8,128)} %param.7) | copy-start | bytes 3145732
  87.9 2.2 %copy-start.1 = (f32[4,8,128]{2,1,0:T(8,128)S(1)}, f32[4,8,128]{2,1,0:T(8,128)}, u32[]{:S(2)}) copy-start(f32[4,8,128]{2,1,0:T(8,128)} %get-tuple-element.5) | copy-start | bytes 49156
where the time goes:
time: 155 us
  Pallas kernels  83.5 us (54%)
  blocking collectives  64.2 us (41%)
  local copies, waits for them, and re-layouts  5.99 us (4%)
    pallas_call x1, Pallas kernels, per_device(): pl.pallas_call(functools.partial(kernel, full_rows, full_cols), name='dec...  83.5 us
    psum x1, blocking collectives, per_device(): total = lax.psum(jnp.sum(squares, axis=(1, 2)), ('ty', 'tx', 'pat'))  64.2 us
    unnamed x6, local copies, waits for them, and re-layouts  4.39 us

commit v1 on v0

--- a/solution.py
+++ b/solution.py
@@ -42,6 +42,7 @@
 def kernel(
     full_rows,
     full_cols,
+    cells,
     est_ref,
     data_ref,
     axial_ref,
@@ -49,7 +50,11 @@
     radius_ref,
     codes_ref,
     out_ref,
+    rms_ref,
     squares_ref,
+    sums_pat,
+    sums_tx,
+    sums_ty,
     grid_ref,
     final_ref,
     home_ref,
@@ -83,6 +88,8 @@
     pat_recv,
     out_send,
     out_recv,
+    sum_send,
+    sum_recv,
 ):
     ty, tx, q = lax.axis_index("ty"), lax.axis_index("tx"), lax.axis_index("pat")
     nty, ntx, npat = lax.axis_size("ty"), lax.axis_size("tx"), lax.axis_size("pat")
@@ -96,24 +103,21 @@
     def peer(d):
         return {"ty": ty, "tx": tx, "pat": lax.rem(q + d, npat)}
 
+    def shifted(dty, dtx, dq):
+        return {
+            "ty": lax.rem(ty + dty + nty, nty),
+            "tx": lax.rem(tx + dtx + ntx, ntx),
+            "pat": lax.rem(q + dq, npat),
+        }
+
     barrier = pltpu.get_barrier_semaphore()
-    greeted = 0
-    for dty in (-1, 0, 1):
-        for dtx in (-1, 0, 1):
-            for dq in range(npat):
-                if dty == 0 and dtx == 0 and dq == 0:
-                    continue
-                pl.semaphore_signal(
-                    barrier,
-                    inc=1,
-                    device_id={
-                        "ty": lax.rem(ty + dty + nty, nty),
-                        "tx": lax.rem(tx + dtx + ntx, ntx),
-                        "pat": lax.rem(q + dq, npat),
-                    },
-                    device_id_type=MESH,
-                )
-                greeted += 1
+    greet = [(a, b, c) for a in (-1, 0, 1) for b in (-1, 0, 1) for c in range(npat)]
+    greet += [(a, 0, 0) for a in range(2, nty - 1)] + [(0, b, 0) for b in range(2, ntx - 1)]
+    greet.remove((0, 0, 0))
+    for move in greet:
+        pl.semaphore_signal(
+            barrier, inc=1, device_id=shifted(*move), device_id_type=MESH
+        )
 
     for strip in range(2):
         for half in range(2):
@@ -122,7 +126,7 @@
                 final_ref[2 * half + k // 4, k % 4, strip] = tile
     grid_ref[0, 1:5, 1:3] = final_ref[q]
 
-    pl.semaphore_wait(barrier, greeted)
+    pl.semaphore_wait(barrier, len(greet))
 
     def halo_copies(t):
         moves = [
@@ -385,7 +389,7 @@
             squares = squares + jnp.where(inner_mask(tile), total, 0.0)
         return squares
 
-    def iteration(t, first):
+    def iteration(t, first, last=False):
         copies = halo_copies(t)
         for copy in copies:
             copy.wait_recv()
@@ -448,6 +452,12 @@
             for strip, chunk in order:
                 squares = compare(strip, chunk, predict(strip, chunk), squares)
         squares_ref[t] = squares
+        if last:
+            share = jnp.zeros((8, LANES), jnp.float32)
+            for k in range(ITERS):
+                total = jnp.sum(squares_ref[k], axis=0, keepdims=True)
+                share = jnp.where(row_iota((8, LANES)) == k, total, share)
+            send_sums(0, share)
         updated = []
         for strip in range(2):
             for chunk in (0, 2):
@@ -472,7 +482,44 @@
                         ]
                     current = grid_ref[t, 1 + chunk + k, 1 + strip]
                     updated.append((chunk + k, strip, current * summed / norm_ref[here]))
+                if last and (strip, chunk) == (0, 2):
+                    send_sums(1, gather_sums(0))
         return updated, copies
+
+    stages = [
+        (sums_pat, npat, q, lambda d: shifted(0, 0, d)),
+        (sums_tx, ntx, tx, lambda d: shifted(0, d, 0)),
+        (sums_ty, nty, ty, lambda d: shifted(d, 0, 0)),
+    ]
+
+    def sum_copies(stage):
+        slots, count, me, device = stages[stage]
+        return [
+            pltpu.make_async_remote_copy(
+                src_ref=slots.at[me],
+                dst_ref=slots.at[me],
+                send_sem=sum_send.at[stage, d - 1],
+                recv_sem=sum_recv.at[stage, d - 1],
+                device_id=device(d),
+                device_id_type=MESH,
+            )
+            for d in range(1, count)
+        ]
+
+    def send_sums(stage, value):
+        slots, _, me, _ = stages[stage]
+        slots[me] = value
+        for copy in sum_copies(stage):
+            copy.start()
+
+    def gather_sums(stage):
+        for copy in sum_copies(stage):
+            copy.wait()
+        slots, count, _, _ = stages[stage]
+        total = slots[0]
+        for k in range(1, count):
+            total = total + slots[k]
+        return total
 
     def edge_in(ref, sem):
         pltpu.make_async_copy(ref, ref, sem).wait()
@@ -494,7 +541,7 @@
     def _(t):
         advance(t, False)
 
-    updated, copies = iteration(ITERS - 1, False)
+    updated, copies = iteration(ITERS - 1, False, True)
     for chunk, strip, value in updated:
         final_ref[q, chunk, strip] = value
     outs = [
@@ -510,6 +557,7 @@
     ]
     for copy in outs:
         copy.start()
+    send_sums(2, gather_sums(1))
     for copy in copies:
         copy.wait_send()
     for copy in outs:
@@ -519,6 +567,8 @@
             tiles = [final_ref[2 * half + k // 4, k % 4, strip] for k in range(8)]
             for y, row in enumerate(block_transpose(tiles)):
                 out_ref[8 * strip + y, :, LANES * half : LANES * (half + 1)] = row
+    total = jnp.sum(gather_sums(2), axis=1, keepdims=True)
+    rms_ref[...] = jnp.broadcast_to(jnp.sqrt(total / cells), (8, LANES))
 
 
 def per_device(estimate, data, axial, lateral_kernel, psf_radius, pattern_codes):
@@ -532,16 +582,21 @@
     smem = pl.BlockSpec(memory_space=pltpu.SMEM)
     f32, bf16 = jnp.float32, jnp.bfloat16
     dma = pltpu.SemaphoreType.DMA
-    rows, squares = pl.pallas_call(
-        functools.partial(kernel, full_rows, full_cols),
+    cells = float(local * lax.axis_size("pat") * planes * full_rows * full_cols)
+    rows, rms = pl.pallas_call(
+        functools.partial(kernel, full_rows, full_cols, cells),
         name="deconvolve",
         out_shape=(
             jax.ShapeDtypeStruct((height, planes, width), f32),
-            jax.ShapeDtypeStruct((ITERS, 8, LANES), f32),
+            jax.ShapeDtypeStruct((8, LANES), f32),
         ),
         in_specs=[vmem, vmem, vmem, smem, smem, smem],
         out_specs=(vmem, vmem),
         scratch_shapes=[
+            pltpu.VMEM((ITERS, 8, LANES), f32),
+            pltpu.VMEM((lax.axis_size("pat"), 8, LANES), f32),
+            pltpu.VMEM((lax.axis_size("tx"), 8, LANES), f32),
+            pltpu.VMEM((lax.axis_size("ty"), 8, LANES), f32),
             pltpu.VMEM((ITERS, 6, 4, 32, LANES), f32),
             pltpu.VMEM((4, 4, 2, 32, LANES), f32),
             pltpu.VMEM((17, 3, 64, LANES), f32),
@@ -575,14 +630,14 @@
             dma((3, 3)),
             dma((3,)),
             dma((3,)),
+            dma((3, 7)),
+            dma((3, 7)),
         ],
         compiler_params=pltpu.CompilerParams(
             collective_id=0, has_side_effects=True, vmem_limit_bytes=56 * 1024 * 1024
         ),
     )(est_rows, data_rows, axial, lateral_kernel, psf_radius, pattern_codes)
-    total = lax.psum(jnp.sum(squares, axis=(1, 2)), ("ty", "tx", "pat"))
-    cells = float(local * lax.axis_size("pat") * planes * full_rows * full_cols)
-    return rows.transpose(1, 0, 2), jnp.sqrt(total / cells)
+    return rows.transpose(1, 0, 2), rms[:ITERS, 0]
 
 
 def solution(mesh):

time: 155 us -> 94.6 us (0.61)
  blocking collectives: 64.2 us -> 0 us
  Pallas kernels: 83.5 us -> 87.2 us
    psum x1 -> x0, blocking collectives: 64.2 us -> none  [per_device(): total = lax.psum(jnp.sum(squares, axis=(1, 2)), ('ty', 'tx', 'pat'))]
    pallas_call x1, Pallas kernels: 83.5 us -> 87.2 us  [per_device(): pl.pallas_call(functools.partial(kernel, full_rows, full_cols, cells), na...]
where the time goes in v1:
time: 94.6 us; the launch traced here: 94.4 us
  Pallas kernels  87.2 us (92%)
  local copies, waits for them, and re-layouts  6.6 us (7%)
    pallas_call x1, Pallas kernels, per_device(): pl.pallas_call(functools.partial(kernel, full_rows, full_cols, cells), na...  87.2 us
    unnamed x6, local copies, waits for them, and re-layouts  4.38 us

profile of v1, /device:TPU:1, one launch (start us, length us, event | category | flops | bytes accessed | tf_op | source)
XLA Modules:
  0.0 94.4 jit_solution(5093690569433027770)
XLA Ops:
  0.6 0.0 copy-start
  0.6 2.2 %copy.15 = f32[32,16,256]{2,0,1:T(8,128)} copy(f32[32,16,256]{2,1,0:T(8,128)} %param.6) | data formatting | bytes 1048576 | tf_op args[0]
  2.9 0.0 copy-done
  2.9 1.6 %copy.12 = f32[16,2,32,256]{3,2,1,0:T(8,128)} copy(f32[16,2,32,256]{3,0,2,1:T(8,128)S(1)} %bitcast.8) | data formatting | bytes 2097152 | tf_op jit(solution)/shard_map/transpose | solution.py:580
  4.5 87.2 %deconvolve.1 = (f32[16,32,256]{2,1,0:T(8,128)}, f32[8,128]{1,0:T(8,128)}) custom-call(f32[16,32,256]{2,1,0:T(8,128)} %bitcast.7, f32[16,64,256]{2,1,0:T(8,128)} %bitcast.6, f32[32,32]{1,0:T(8,128)} %axial_ref.1, f32[9,9]{1,0:T(8,128)} %taps_ref.1, s32[9]{0:T(128)} %radius_ref.1, s32[2,8]{1,0:T(2,128)} %codes_ref.1), custom_call_target="tpu_custom_call" | custom-call | tf_op jit(solution)/shard_map/deconvolve/pallas_call | solution.py:586
  91.7 0.0 copy-start.1
  91.7 2.1 %copy.13 = f32[32,16,256]{2,1,0:T(8,128)} copy(f32[32,16,256]{2,0,1:T(8,128)} %bitcast.9) | data formatting | bytes 1048576
  93.8 0.0 copy-done.1
  93.8 0.6 slice_reduce_fusion
Async XLA Ops:
  0.6 2.2 %copy-start = (f32[2,32,16,256]{3,2,1,0:T(8,128)S(1)}, f32[2,32,16,256]{3,2,1,0:T(8,128)}, u32[]{:S(2)}) copy-start(f32[2,32,16,256]{3,2,1,0:T(8,128)} %param.7) | copy-start | bytes 3145732
  91.7 2.2 %copy-start.1 = (f32[8,128]{1,0:T(8,128)S(1)}, f32[8,128]{1,0:T(8,128)}, u32[]{:S(2)}) copy-start(f32[8,128]{1,0:T(8,128)} %get-tuple-element.5) | copy-start | bytes 12292

commit v2 on v1

--- a/solution.py
+++ b/solution.py
@@ -52,8 +52,7 @@
     out_ref,
     rms_ref,
     squares_ref,
-    sums_pat,
-    sums_tx,
+    sums_row,
     sums_ty,
     grid_ref,
     final_ref,
@@ -94,14 +93,21 @@
     ty, tx, q = lax.axis_index("ty"), lax.axis_index("tx"), lax.axis_index("pat")
     nty, ntx, npat = lax.axis_size("ty"), lax.axis_size("tx"), lax.axis_size("pat")
     ncol = ntx * npat
-    column = tx * npat + q
+
+    def turned(tile, place):
+        return jnp.where(lax.rem(tile, 2) == 0, place, npat - 1 - place)
+
+    mine = turned(tx, q)
+    column = tx * npat + mine
 
     def at(dty, dcol):
         c = lax.rem(column + dcol + ncol, ncol)
-        return {"ty": lax.rem(ty + dty + nty, nty), "tx": c // npat, "pat": lax.rem(c, npat)}
-
-    def peer(d):
-        return {"ty": ty, "tx": tx, "pat": lax.rem(q + d, npat)}
+        tile = c // npat
+        return {
+            "ty": lax.rem(ty + dty + nty, nty),
+            "tx": tile,
+            "pat": turned(tile, lax.rem(c, npat)),
+        }
 
     def shifted(dty, dtx, dq):
         return {
@@ -110,9 +116,13 @@
             "pat": lax.rem(q + dq, npat),
         }
 
+    def peer(d):
+        return shifted(0, 0, d)
+
     barrier = pltpu.get_barrier_semaphore()
-    greet = [(a, b, c) for a in (-1, 0, 1) for b in (-1, 0, 1) for c in range(npat)]
-    greet += [(a, 0, 0) for a in range(2, nty - 1)] + [(0, b, 0) for b in range(2, ntx - 1)]
+    greet = [(0, b, c) for b in range(ntx) for c in range(npat)]
+    greet += [(a, b, c) for a in (-1, 1) for b in (-1, 0, 1) for c in range(npat)]
+    greet += [(a, 0, 0) for a in range(2, nty - 1)]
     greet.remove((0, 0, 0))
     for move in greet:
         pl.semaphore_signal(
@@ -124,23 +134,28 @@
             rows = [est_ref[8 * strip + y, :, LANES * half : LANES * (half + 1)] for y in range(8)]
             for k, tile in enumerate(block_transpose(rows)):
                 final_ref[2 * half + k // 4, k % 4, strip] = tile
-    grid_ref[0, 1:5, 1:3] = final_ref[q]
-
-    pl.semaphore_wait(barrier, len(greet))
-
-    def halo_copies(t):
-        moves = [
-            ((slice(1, 5), 1), (slice(1, 5), 3), -1, 0),
-            ((slice(1, 5), 2), (slice(1, 5), 0), 1, 0),
-            ((1, slice(1, 3)), (5, slice(1, 3)), 0, -1),
-            ((4, slice(1, 3)), (0, slice(1, 3)), 0, 1),
-            ((1, 1), (5, 3), -1, -1),
-            ((4, 1), (0, 3), -1, 1),
-            ((1, 2), (5, 0), 1, -1),
-            ((4, 2), (0, 0), 1, 1),
-        ]
+    grid_ref[0, 1:5, 1:3] = final_ref[mine]
+
+    moves = [
+        ((slice(1, 5), 1), (slice(1, 5), 3), -1, 0),
+        ((slice(1, 5), 2), (slice(1, 5), 0), 1, 0),
+        ((1, 1), (5, 1), 0, -1),
+        ((4, 1), (0, 1), 0, 1),
+        ((1, 2), (5, 2), 0, -1),
+        ((4, 2), (0, 2), 0, 1),
+        ((1, 1), (5, 3), -1, -1),
+        ((4, 1), (0, 3), -1, 1),
+        ((1, 2), (5, 0), 1, -1),
+        ((4, 2), (0, 0), 1, 1),
+    ]
+    from_strip = ((2, 3, 0, 6, 7), (4, 5, 1, 8, 9))
+    side_halo = (2, 3, 4, 5)
+    row_halo = {0: (1, 8, 9), 3: (0, 6, 7)}
+
+    def halo_copies(t, which):
         copies = []
-        for k, (source, target, dty, dcol) in enumerate(moves):
+        for k in which:
+            source, target, dty, dcol = moves[k]
             copies.append(
                 pltpu.make_async_remote_copy(
                     src_ref=grid_ref.at[(t, *source)],
@@ -152,9 +167,6 @@
                 )
             )
         return copies
-
-    for copy in halo_copies(0):
-        copy.start()
 
     row_copies = [
         pltpu.make_async_remote_copy(
@@ -174,9 +186,6 @@
             device_id_type=MESH,
         ),
     ]
-    for copy in row_copies:
-        copy.start()
-
     def data_row(row, block, half):
         rows = slice(8 * block, 8 * block + 8)
         lanes = slice(LANES * half, LANES * (half + 1))
@@ -206,7 +215,7 @@
     def strip_copies(strip):
         copies = []
         for d in range(1, npat):
-            to = lax.rem(q + d, npat)
+            to = turned(tx, lax.rem(q + d, npat))
             copies.append(
                 pltpu.make_async_remote_copy(
                     src_ref=home_ref.at[pl.ds(4 * to, 5), strip],
@@ -219,51 +228,78 @@
             )
         return copies
 
-    def edge_copies():
+    def edge_copies(strip):
+        after, before = lax.rem(tx + 1, ntx), lax.rem(tx + ntx - 1, ntx)
         return [
             pltpu.make_async_remote_copy(
-                src_ref=home_ref.at[16],
-                dst_ref=left_ref.at[q],
-                send_sem=edge_send.at[0],
-                recv_sem=left_recv.at[q],
-                device_id={"ty": ty, "tx": lax.rem(tx + 1, ntx), "pat": 0},
+                src_ref=home_ref.at[16, strip],
+                dst_ref=left_ref.at[q, strip],
+                send_sem=edge_send.at[0, strip],
+                recv_sem=left_recv.at[q, strip],
+                device_id={"ty": ty, "tx": after, "pat": turned(after, 0)},
                 device_id_type=MESH,
             ),
             pltpu.make_async_remote_copy(
-                src_ref=home_ref.at[0],
-                dst_ref=right_ref.at[q],
-                send_sem=edge_send.at[1],
-                recv_sem=right_recv.at[q],
-                device_id={"ty": ty, "tx": lax.rem(tx + ntx - 1, ntx), "pat": npat - 1},
+                src_ref=home_ref.at[0, strip],
+                dst_ref=right_ref.at[q, strip],
+                send_sem=edge_send.at[1, strip],
+                recv_sem=right_recv.at[q, strip],
+                device_id={"ty": ty, "tx": before, "pat": turned(before, npat - 1)},
                 device_id_type=MESH,
             ),
         ]
 
     make_strip(1)
-    for copy in strip_copies(1):
+    pl.semaphore_wait(barrier, len(greet))
+    for copy in row_copies + halo_copies(0, side_halo):
         copy.start()
-
-    lane = lane_iota((LANES, LANES))
-    line = row_iota((LANES, LANES))
+    for copy in strip_copies(1) + edge_copies(1):
+        copy.start()
+    for copy in halo_copies(0, row_halo[0] + row_halo[3]):
+        copy.start()
+
+    taps = [
+        [jnp.where(abs(j - 4) <= radius_ref[i], taps_ref[i, j], 0.0) for j in range(TAPS)]
+        for i in range(TAPS)
+    ]
+    narrow = (16, LANES)
+    group = lane_iota(narrow) // 16
     for backward in (False, True):
         target = adjoint_ref if backward else forward_ref
-        target[...] = jnp.zeros_like(target)
-        for block in range(2):
-            row_gap = 8 * block + line // 16 - lane // 16
-            for step in range(2):
-                col_gap = 16 * step + lax.rem(line, 16) - lax.rem(lane, 16)
-                total = jnp.zeros((LANES, LANES), jnp.float32)
-                for i in range(TAPS):
-                    here = jnp.zeros((LANES, LANES), jnp.float32)
-                    for j in range(TAPS):
-                        ki, kj = (TAPS - 1 - i, TAPS - 1 - j) if backward else (i, j)
-                        tap = jnp.where(abs(kj - 4) <= radius_ref[ki], taps_ref[ki, kj], 0.0)
-                        here = jnp.where(col_gap == j, tap, here)
-                    total = jnp.where(row_gap == i, here, total)
-                values = total.astype(jnp.bfloat16)
-                for out_chunk in range(2):
-                    start = 256 * (out_chunk + step) + LANES * block
-                    target[start : start + LANES, LANES * out_chunk : LANES * (out_chunk + 1)] = values
+        target[0:256, LANES:] = jnp.zeros((256, LANES), jnp.bfloat16)
+        target[512:768, 0:LANES] = jnp.zeros((256, LANES), jnp.bfloat16)
+
+        def tap(i, j):
+            return taps[TAPS - 1 - i][TAPS - 1 - j] if backward else taps[i][j]
+
+        for step in range(2):
+            gap = 16 * step + row_iota(narrow) - lane_iota(narrow) % 16
+            low = jnp.zeros(narrow, jnp.float32)
+            high = jnp.zeros(narrow, jnp.float32)
+            for j in range(TAPS):
+                values = jnp.zeros(narrow, jnp.float32)
+                for g in range(8):
+                    values = jnp.where(group == g, tap(7 - g, j), values)
+                high = jnp.where(gap == j, values, high)
+                low = jnp.where((gap == j) & (group == 7), tap(8, j), low)
+            for block in range(2):
+                for y in range(8):
+                    if block:
+                        first = 7 - y
+                        left, right = low, high
+                    else:
+                        first = 7 - y
+                        left, right = high, None
+                    turn = (LANES - 16 * first) % LANES
+                    left = pltpu.roll(left, turn, 1) if turn else left
+                    if right is None:
+                        right = jnp.zeros(narrow, jnp.float32)
+                    else:
+                        right = pltpu.roll(right, turn, 1) if turn else right
+                    values = jnp.where(group < 8 - first, left, right).astype(jnp.bfloat16)
+                    for out_chunk in range(2):
+                        start = 256 * (out_chunk + step) + LANES * block + 16 * y
+                        target[start : start + 16, LANES * out_chunk : LANES * (out_chunk + 1)] = values
 
     spread = (row_iota((256, 32)) % 32 == lane_iota((256, 32))).astype(jnp.bfloat16)
     axial_b = axial_ref[...].astype(jnp.bfloat16)
@@ -275,6 +311,14 @@
     left_adj = lax.dot_general(spread, axial_b, nt, preferred_element_type=jnp.float32)
     full = lax.dot_general(left_adj.astype(jnp.bfloat16), spread, nt, preferred_element_type=jnp.float32)
     axial_adj[...] = jnp.where(same, full, 0.0).astype(jnp.bfloat16)
+
+    for copy in row_copies:
+        copy.wait_recv()
+    for strip in (2, 0):
+        make_strip(strip)
+        for copy in strip_copies(strip) + edge_copies(strip):
+            copy.start()
+    data_tiles[q] = home_ref[pl.ds(4 * mine, 5)]
 
     plane = row_iota((32, LANES)).astype(jnp.float32)
     planes_ref[...] = jnp.cos(plane * (2.0 * math.pi * 3.0 / 32.0))
@@ -317,14 +361,6 @@
     tile15 = (16, LANES)
     valid = inside(tile15, 3, 4) & ((row_iota(tile15) < 12) | (lane_iota(tile15) % 16 < 8))
     valid_ref[...] = valid.astype(jnp.float32)
-
-    for copy in row_copies:
-        copy.wait_recv()
-    make_strip(0)
-    make_strip(2)
-    for copy in strip_copies(0) + strip_copies(2) + edge_copies():
-        copy.start()
-    data_tiles[q] = home_ref[pl.ds(4 * q, 5)]
 
     column_sum = lax.dot_general(
         axial_b, jnp.ones((32, LANES), jnp.bfloat16), (((0,), (0,)), ((), ())),
@@ -389,106 +425,8 @@
             squares = squares + jnp.where(inner_mask(tile), total, 0.0)
         return squares
 
-    def iteration(t, first, last=False):
-        copies = halo_copies(t)
-        for copy in copies:
-            copy.wait_recv()
-        wave_z = planes_ref[...]
-        left_half = lane_iota((32, LANES)) % 16 < 8
-        for chunk in range(5):
-            for strip in range(4):
-                tile = 4 * chunk + strip
-                a, b = grid_ref[t, chunk, strip], grid_ref[t, chunk + 1, strip]
-                value = jnp.where(left_half, pltpu.roll(a, LANES - 8, 1), pltpu.roll(b, 8, 1))
-                value = value * mask_ext[tile : tile + 1, :]
-                for p in range(NPAT):
-                    light = 1.0 + wave_ext[NPAT * tile + p : NPAT * tile + p + 1, :] * wave_z
-                    lit_ref[32 * p : 32 * (p + 1), LANES * tile : LANES * (tile + 1)] = (
-                        light * value
-                    ).astype(jnp.bfloat16)
-        for pair in range(10):
-            lanes = slice(256 * pair, 256 * (pair + 1))
-            blur_ref[:, lanes] = jnp.dot(
-                axial_fwd[...], lit_ref[:, lanes], preferred_element_type=jnp.float32
-            ).astype(jnp.bfloat16)
-        squares = jnp.zeros((8, LANES), jnp.float32)
-        order = [(strip, chunk) for strip in range(3) for chunk in (0, 2, 4)]
-        if first:
-            for strip, chunk in order:
-                width = LANES if chunk == 4 else 2 * LANES
-                tile = 5 * strip + chunk
-                pred_ref[:, LANES * tile : LANES * tile + width] = predict(strip, chunk)
-            for strip in range(3):
-                for copy in strip_copies(strip):
-                    copy.wait_recv()
-
-            @pl.when(q == 0)
-            def _():
-                for source in range(4):
-                    edge_in(left_ref.at[source], left_recv.at[source])
-                    keep = lane_iota((64, LANES)) % 16 < 4
-                    for strip in range(3):
-                        data_tiles[source, 0, strip] = jnp.where(
-                            keep, left_ref[source, strip], data_tiles[source, 0, strip]
-                        )
-
-            @pl.when(q == npat - 1)
-            def _():
-                for source in range(4):
-                    edge_in(right_ref.at[source], right_recv.at[source])
-                    keep = lane_iota((64, LANES)) % 16 < 4
-                    for strip in range(3):
-                        data_tiles[source, 4, strip] = jnp.where(
-                            keep, data_tiles[source, 4, strip], right_ref[source, strip]
-                        )
-
-            for strip, chunk in order:
-                width = LANES if chunk == 4 else 2 * LANES
-                tile = 5 * strip + chunk
-                squares = compare(
-                    strip, chunk, pred_ref[:, LANES * tile : LANES * tile + width], squares
-                )
-        else:
-            for strip, chunk in order:
-                squares = compare(strip, chunk, predict(strip, chunk), squares)
-        squares_ref[t] = squares
-        if last:
-            share = jnp.zeros((8, LANES), jnp.float32)
-            for k in range(ITERS):
-                total = jnp.sum(squares_ref[k], axis=0, keepdims=True)
-                share = jnp.where(row_iota((8, LANES)) == k, total, share)
-            send_sums(0, share)
-        updated = []
-        for strip in range(2):
-            for chunk in (0, 2):
-                tile = 3 * chunk + strip
-                window = jnp.concatenate(
-                    [quot_ref[:, LANES * (tile + 3 * k) : LANES * (tile + 3 * k + 2)] for k in range(3)],
-                    axis=1,
-                )
-                spread_back = jnp.dot(
-                    window, adjoint_ref[...], preferred_element_type=jnp.float32
-                ).astype(jnp.bfloat16)
-                gathered = jnp.dot(
-                    axial_adj[...], spread_back, preferred_element_type=jnp.float32
-                )
-                for k in range(2):
-                    here = 2 * (chunk + k) + strip
-                    summed = jnp.zeros((32, LANES), jnp.float32)
-                    for p in range(NPAT):
-                        light = 1.0 + wave_in[NPAT * here + p : NPAT * here + p + 1, :] * wave_z
-                        summed = summed + light * gathered[
-                            32 * p : 32 * (p + 1), LANES * k : LANES * (k + 1)
-                        ]
-                    current = grid_ref[t, 1 + chunk + k, 1 + strip]
-                    updated.append((chunk + k, strip, current * summed / norm_ref[here]))
-                if last and (strip, chunk) == (0, 2):
-                    send_sums(1, gather_sums(0))
-        return updated, copies
-
     stages = [
-        (sums_pat, npat, q, lambda d: shifted(0, 0, d)),
-        (sums_tx, ntx, tx, lambda d: shifted(0, d, 0)),
+        (sums_row, ncol, tx * npat + q, lambda d: shifted(0, d // npat, d % npat)),
         (sums_ty, nty, ty, lambda d: shifted(d, 0, 0)),
     ]
 
@@ -521,53 +459,174 @@
             total = total + slots[k]
         return total
 
-    def edge_in(ref, sem):
+    def lit_tiles(t, strips):
+        wave_z = planes_ref[...]
+        left_half = lane_iota((32, LANES)) % 16 < 8
+        for chunk in range(5):
+            for strip in strips:
+                tile = 4 * chunk + strip
+                a, b = grid_ref[t, chunk, strip], grid_ref[t, chunk + 1, strip]
+                value = jnp.where(left_half, pltpu.roll(a, LANES - 8, 1), pltpu.roll(b, 8, 1))
+                value = value * mask_ext[tile : tile + 1, :]
+                for p in range(NPAT):
+                    light = 1.0 + wave_ext[NPAT * tile + p : NPAT * tile + p + 1, :] * wave_z
+                    lit_ref[32 * p : 32 * (p + 1), LANES * tile : LANES * (tile + 1)] = (
+                        light * value
+                    ).astype(jnp.bfloat16)
+        tiles = [4 * chunk + strip for chunk in range(5) for strip in strips]
+        for k in range(0, len(tiles), 2):
+            pair = [slice(LANES * tile, LANES * (tile + 1)) for tile in tiles[k : k + 2]]
+            lit = jnp.concatenate([lit_ref[:, lanes] for lanes in pair], axis=1)
+            blurred = jnp.dot(axial_fwd[...], lit, preferred_element_type=jnp.float32)
+            for n, lanes in enumerate(pair):
+                blur_ref[:, lanes] = blurred[:, LANES * n : LANES * (n + 1)].astype(jnp.bfloat16)
+
+    def wait_halo(t, which):
+        for copy in halo_copies(t, which):
+            copy.wait_recv()
+
+    def wait_data(strip):
+        for copy in strip_copies(strip):
+            copy.wait_recv()
+        keep = lane_iota((64, LANES)) % 16 < 4
+
+        @pl.when(mine == 0)
+        def _():
+            for source in range(4):
+                arrived(left_ref.at[source, strip], left_recv.at[source, strip])
+                data_tiles[source, 0, strip] = jnp.where(
+                    keep, left_ref[source, strip], data_tiles[source, 0, strip]
+                )
+
+        @pl.when(mine == npat - 1)
+        def _():
+            for source in range(4):
+                arrived(right_ref.at[source, strip], right_recv.at[source, strip])
+                data_tiles[source, 4, strip] = jnp.where(
+                    keep, data_tiles[source, 4, strip], right_ref[source, strip]
+                )
+
+    def arrived(ref, sem):
         pltpu.make_async_copy(ref, ref, sem).wait()
 
-    def advance(t, first):
-        updated, copies = iteration(t, first)
-        for chunk, strip, value in updated:
-            grid_ref[t + 1, 1 + chunk, 1 + strip] = value
-        for copy in halo_copies(t + 1):
+    def back_project(t, strip):
+        wave_z = planes_ref[...]
+        updated = []
+        for chunk in (0, 2):
+            tile = 3 * chunk + strip
+            window = jnp.concatenate(
+                [quot_ref[:, LANES * (tile + 3 * k) : LANES * (tile + 3 * k + 2)] for k in range(3)],
+                axis=1,
+            )
+            spread_back = jnp.dot(
+                window, adjoint_ref[...], preferred_element_type=jnp.float32
+            ).astype(jnp.bfloat16)
+            gathered = jnp.dot(axial_adj[...], spread_back, preferred_element_type=jnp.float32)
+            for k in range(2):
+                here = 2 * (chunk + k) + strip
+                summed = jnp.zeros((32, LANES), jnp.float32)
+                for p in range(NPAT):
+                    light = 1.0 + wave_in[NPAT * here + p : NPAT * here + p + 1, :] * wave_z
+                    summed = summed + light * gathered[
+                        32 * p : 32 * (p + 1), LANES * k : LANES * (k + 1)
+                    ]
+                current = grid_ref[t, 1 + chunk + k, 1 + strip]
+                updated.append((chunk + k, current * summed / norm_ref[here]))
+        return updated
+
+    def out_copies(strip):
+        return [
+            pltpu.make_async_remote_copy(
+                src_ref=final_ref.at[mine, :, strip],
+                dst_ref=final_ref.at[mine, :, strip],
+                send_sem=out_send.at[strip, d - 1],
+                recv_sem=out_recv.at[strip, d - 1],
+                device_id=peer(d),
+                device_id_type=MESH,
+            )
+            for d in range(1, npat)
+        ]
+
+    def compare_strip(t, strip, squares):
+        for chunk in (0, 2, 4):
+            if t == 0:
+                width = LANES if chunk == 4 else 2 * LANES
+                tile = 5 * strip + chunk
+                predicted = pred_ref[:, LANES * tile : LANES * tile + width]
+            else:
+                predicted = predict(strip, chunk)
+            squares = compare(strip, chunk, predicted, squares)
+        return squares
+
+    def finish_strip(t, strip):
+        for chunk, value in back_project(t, strip):
+            if t == ITERS - 1:
+                final_ref[mine, chunk, strip] = value
+            else:
+                grid_ref[t + 1, 1 + chunk, 1 + strip] = value
+        if t == ITERS - 1:
+            copies = out_copies(strip)
+        else:
+            copies = halo_copies(t + 1, from_strip[strip])
+        for copy in copies:
             copy.start()
-        for copy in copies:
+
+    for t in range(ITERS):
+        early = 1 - t % 2
+        near, far = (2, 0) if early == 1 else (0, 2)
+        near_halo, far_halo = (3, 0) if early == 1 else (0, 3)
+        squares = jnp.zeros((8, LANES), jnp.float32)
+        wait_halo(t, side_halo)
+        lit_tiles(t, (1, 2))
+        if t == 0:
+            wait_halo(t, row_halo[0] + row_halo[3])
+            lit_tiles(t, (0, 3))
+            for strip in range(3):
+                for chunk in (0, 2, 4):
+                    width = LANES if chunk == 4 else 2 * LANES
+                    tile = 5 * strip + chunk
+                    pred_ref[:, LANES * tile : LANES * tile + width] = predict(strip, chunk)
+            wait_data(1)
+        squares = compare_strip(t, 1, squares)
+        if t == 0:
+            wait_data(near)
+        else:
+            wait_halo(t, row_halo[near_halo])
+            lit_tiles(t, (near_halo,))
+        squares = compare_strip(t, near, squares)
+        finish_strip(t, early)
+        if t == 0:
+            wait_data(far)
+        else:
+            wait_halo(t, row_halo[far_halo])
+            lit_tiles(t, (far_halo,))
+        squares = compare_strip(t, far, squares)
+        squares_ref[t] = squares
+        if t == ITERS - 1:
+            share = jnp.zeros((8, LANES), jnp.float32)
+            for k in range(ITERS):
+                total = jnp.sum(squares_ref[k], axis=0, keepdims=True)
+                share = jnp.where(row_iota((8, LANES)) == k, total, share)
+            send_sums(0, share)
+        finish_strip(t, 1 - early)
+
+    send_sums(1, gather_sums(0))
+    for copy in row_copies:
+        copy.wait_send()
+    for strip in range(3):
+        for copy in strip_copies(strip) + edge_copies(strip):
             copy.wait_send()
-
-    advance(0, True)
-    for copy in row_copies + strip_copies(0) + strip_copies(1) + strip_copies(2) + edge_copies():
-        copy.wait_send()
-
-    @pl.loop(1, ITERS - 1)
-    def _(t):
-        advance(t, False)
-
-    updated, copies = iteration(ITERS - 1, False, True)
-    for chunk, strip, value in updated:
-        final_ref[q, chunk, strip] = value
-    outs = [
-        pltpu.make_async_remote_copy(
-            src_ref=final_ref.at[q],
-            dst_ref=final_ref.at[q],
-            send_sem=out_send.at[d - 1],
-            recv_sem=out_recv.at[d - 1],
-            device_id=peer(d),
-            device_id_type=MESH,
-        )
-        for d in range(1, npat)
-    ]
-    for copy in outs:
-        copy.start()
-    send_sums(2, gather_sums(1))
-    for copy in copies:
-        copy.wait_send()
-    for copy in outs:
-        copy.wait()
-    for strip in range(2):
+    for t in range(ITERS):
+        for copy in halo_copies(t, range(len(moves))):
+            copy.wait_send()
+    for strip in (early, 1 - early):
+        for copy in out_copies(strip):
+            copy.wait()
         for half in range(2):
             tiles = [final_ref[2 * half + k // 4, k % 4, strip] for k in range(8)]
             for y, row in enumerate(block_transpose(tiles)):
                 out_ref[8 * strip + y, :, LANES * half : LANES * (half + 1)] = row
-    total = jnp.sum(gather_sums(2), axis=1, keepdims=True)
+    total = jnp.sum(gather_sums(1), axis=1, keepdims=True)
     rms_ref[...] = jnp.broadcast_to(jnp.sqrt(total / cells), (8, LANES))
 
 
@@ -594,8 +653,7 @@
         out_specs=(vmem, vmem),
         scratch_shapes=[
             pltpu.VMEM((ITERS, 8, LANES), f32),
-            pltpu.VMEM((lax.axis_size("pat"), 8, LANES), f32),
-            pltpu.VMEM((lax.axis_size("tx"), 8, LANES), f32),
+            pltpu.VMEM((lax.axis_size(("tx", "pat")), 8, LANES), f32),
             pltpu.VMEM((lax.axis_size("ty"), 8, LANES), f32),
             pltpu.VMEM((ITERS, 6, 4, 32, LANES), f32),
             pltpu.VMEM((4, 4, 2, 32, LANES), f32),
@@ -619,19 +677,19 @@
             pltpu.VMEM((24, LANES), f32),
             pltpu.VMEM((16, LANES), f32),
             pltpu.VMEM((8, 32, LANES), f32),
-            dma((ITERS, 8)),
-            dma((ITERS, 8)),
+            dma((ITERS, 10)),
+            dma((ITERS, 10)),
             dma((2,)),
             dma((2,)),
-            dma((2,)),
-            dma((4,)),
-            dma((4,)),
+            dma((2, 3)),
+            dma((4, 3)),
+            dma((4, 3)),
             dma((3, 3)),
             dma((3, 3)),
-            dma((3,)),
-            dma((3,)),
-            dma((3, 7)),
-            dma((3, 7)),
+            dma((2, 3)),
+            dma((2, 3)),
+            dma((2, 15)),
+            dma((2, 15)),
         ],
         compiler_params=pltpu.CompilerParams(
             collective_id=0, has_side_effects=True, vmem_limit_bytes=56 * 1024 * 1024

time: 94.6 us -> 81 us (0.86)
  Pallas kernels: 87.2 us -> 73.6 us
    pallas_call x1, Pallas kernels: 87.2 us -> 73.6 us  [per_device(): pl.pallas_call(functools.partial(kernel, full_rows, full_cols, cells), na...]
where the time goes in v2:
time: 81 us; the launch traced here: 80.8 us
  Pallas kernels  73.6 us (91%)
  local copies, waits for them, and re-layouts  6.6 us (8%)
    pallas_call x1, Pallas kernels, per_device(): pl.pallas_call(functools.partial(kernel, full_rows, full_cols, cells), na...  73.6 us
    unnamed x6, local copies, waits for them, and re-layouts  4.38 us

profile of v2, /device:TPU:1, one launch (start us, length us, event | category | flops | bytes accessed | tf_op | source)
XLA Modules:
  0.0 80.8 jit_solution(5223307782394411760)
XLA Ops:
  0.6 0.0 copy-start
  0.6 2.2 %copy.15 = f32[32,16,256]{2,0,1:T(8,128)} copy(f32[32,16,256]{2,1,0:T(8,128)} %param.6) | data formatting | bytes 1048576 | tf_op args[0]
  2.9 0.0 copy-done
  2.9 1.6 %copy.12 = f32[16,2,32,256]{3,2,1,0:T(8,128)} copy(f32[16,2,32,256]{3,0,2,1:T(8,128)S(1)} %bitcast.8) | data formatting | bytes 2097152 | tf_op jit(solution)/shard_map/transpose | solution.py:639
  4.5 73.6 %deconvolve.1 = (f32[16,32,256]{2,1,0:T(8,128)}, f32[8,128]{1,0:T(8,128)}) custom-call(f32[16,32,256]{2,1,0:T(8,128)} %bitcast.7, f32[16,64,256]{2,1,0:T(8,128)} %bitcast.6, f32[32,32]{1,0:T(8,128)} %axial_ref.1, f32[9,9]{1,0:T(8,128)} %taps_ref.1, s32[9]{0:T(128)} %radius_ref.1, s32[2,8]{1,0:T(2,128)} %codes_ref.1), custom_call_target="tpu_custom_call" | custom-call | tf_op jit(solution)/shard_map/deconvolve/pallas_call | solution.py:645
  78.0 0.0 copy-start.1
  78.0 2.1 %copy.13 = f32[32,16,256]{2,1,0:T(8,128)} copy(f32[32,16,256]{2,0,1:T(8,128)} %bitcast.9) | data formatting | bytes 1048576
  80.2 0.0 copy-done.1
  80.2 0.6 slice_reduce_fusion
Async XLA Ops:
  0.6 2.2 %copy-start = (f32[2,32,16,256]{3,2,1,0:T(8,128)S(1)}, f32[2,32,16,256]{3,2,1,0:T(8,128)}, u32[]{:S(2)}) copy-start(f32[2,32,16,256]{3,2,1,0:T(8,128)} %param.7) | copy-start | bytes 3145732
  78.0 2.2 %copy-start.1 = (f32[8,128]{1,0:T(8,128)S(1)}, f32[8,128]{1,0:T(8,128)}, u32[]{:S(2)}) copy-start(f32[8,128]{1,0:T(8,128)} %get-tuple-element.5) | copy-start | bytes 12292

commit v3 on v2

--- a/solution.py
+++ b/solution.py
@@ -54,12 +54,18 @@
     squares_ref,
     sums_row,
     sums_ty,
+    est_rows,
+    data_rows,
+    out_rows,
+    load_sem,
+    store_sem,
     grid_ref,
     final_ref,
     home_ref,
-    data_tiles,
-    top_ref,
-    bottom_ref,
+    data_in,
+    data_mid,
+    relay_out,
+    relay_in,
     left_ref,
     right_ref,
     lit_ref,
@@ -78,8 +84,8 @@
     norm_ref,
     halo_send,
     halo_recv,
-    row_send,
-    row_recv,
+    relay_send,
+    relay_recv,
     edge_send,
     left_recv,
     right_recv,
@@ -93,6 +99,15 @@
     ty, tx, q = lax.axis_index("ty"), lax.axis_index("tx"), lax.axis_index("pat")
     nty, ntx, npat = lax.axis_size("ty"), lax.axis_size("tx"), lax.axis_size("pat")
     ncol = ntx * npat
+    loads = [
+        pltpu.make_async_copy(
+            source.at[:, LANES * half : LANES * (half + 1)], target.at[half], load_sem.at[k, half]
+        )
+        for k, (source, target) in enumerate(((est_ref, est_rows), (data_ref, data_rows)))
+        for half in range(2)
+    ]
+    for copy in loads:
+        copy.start()
 
     def turned(tile, place):
         return jnp.where(lax.rem(tile, 2) == 0, place, npat - 1 - place)
@@ -129,9 +144,11 @@
             barrier, inc=1, device_id=shifted(*move), device_id_type=MESH
         )
 
+    for half in range(2):
+        loads[half].wait()
     for strip in range(2):
         for half in range(2):
-            rows = [est_ref[8 * strip + y, :, LANES * half : LANES * (half + 1)] for y in range(8)]
+            rows = [est_rows[half, pl.ds(8 * strip + y, 32, stride=16)] for y in range(8)]
             for k, tile in enumerate(block_transpose(rows)):
                 final_ref[2 * half + k // 4, k % 4, strip] = tile
     grid_ref[0, 1:5, 1:3] = final_ref[mine]
@@ -168,95 +185,141 @@
             )
         return copies
 
-    row_copies = [
-        pltpu.make_async_remote_copy(
-            src_ref=data_ref.at[12:16],
-            dst_ref=top_ref,
-            send_sem=row_send.at[0],
-            recv_sem=row_recv.at[0],
-            device_id=at(1, 0),
-            device_id_type=MESH,
-        ),
-        pltpu.make_async_remote_copy(
-            src_ref=data_ref.at[0:4],
-            dst_ref=bottom_ref,
-            send_sem=row_send.at[1],
-            recv_sem=row_recv.at[1],
-            device_id=at(-1, 0),
-            device_id_type=MESH,
-        ),
-    ]
-    def data_row(row, block, half):
-        rows = slice(8 * block, 8 * block + 8)
-        lanes = slice(LANES * half, LANES * (half + 1))
-        if row < 4:
-            return top_ref[row, rows, lanes]
-        if row < 20:
-            return data_ref[row - 4, rows, lanes]
-        return bottom_ref[row - 20, rows, lanes]
-
-    def make_strip(strip):
+    kind_rows = (range(4, 12), (12, 13, 14, 15, 0, 1, 2, 3))
+
+    def make_strip(kind):
         first = lane_iota((8, LANES)) < 4
+        group = lane_iota((8, LANES)) // 16
         for block in range(8):
             at_rows = slice(8 * block, 8 * block + 8)
-            low = [pltpu.roll(data_row(8 * strip + y, block, 0), 4, 1) for y in range(8)]
-            high = [pltpu.roll(data_row(8 * strip + y, block, 1), 4, 1) for y in range(8)]
+
+            def rows_of(half):
+                return [
+                    pltpu.roll(data_rows[half, pl.ds(128 * block + y, 8, stride=16)], 4, 1)
+                    for y in kind_rows[kind]
+                ]
+
+            low, high = rows_of(0), rows_of(1)
             for k, tile in enumerate(block_transpose(low)):
-                home_ref[k, strip, at_rows] = tile
+                home_ref[k, kind, at_rows] = tile
             mixed = [jnp.where(first, a, b) for a, b in zip(low, high)]
             for k, tile in enumerate(block_transpose(mixed)):
-                home_ref[8 + k, strip, at_rows] = tile
+                home_ref[8 + k, kind, at_rows] = tile
             last = high[0]
-            group = lane_iota((8, LANES)) // 16
             for y in range(1, 8):
                 last = jnp.where(group == y, pltpu.roll(high[y], 16 * y, 1), last)
-            home_ref[16, strip, at_rows] = last
-
-    def strip_copies(strip):
-        copies = []
-        for d in range(1, npat):
-            to = turned(tx, lax.rem(q + d, npat))
-            copies.append(
-                pltpu.make_async_remote_copy(
-                    src_ref=home_ref.at[pl.ds(4 * to, 5), strip],
-                    dst_ref=data_tiles.at[q, :, strip],
-                    send_sem=pat_send.at[strip, d - 1],
-                    recv_sem=pat_recv.at[strip, d - 1],
-                    device_id=peer(d),
-                    device_id_type=MESH,
-                )
-            )
-        return copies
-
-    def edge_copies(strip):
+            home_ref[16, kind, at_rows] = last
+
+    def strip_copy(kind, d):
+        to = turned(tx, lax.rem(q + d, npat))
+        return pltpu.make_async_remote_copy(
+            src_ref=home_ref.at[pl.ds(4 * to, 5), kind],
+            dst_ref=data_in.at[q, :, kind],
+            send_sem=pat_send.at[kind, d - 1],
+            recv_sem=pat_recv.at[kind, d - 1],
+            device_id=peer(d),
+            device_id_type=MESH,
+        )
+
+    def edge_copies(kind):
         after, before = lax.rem(tx + 1, ntx), lax.rem(tx + ntx - 1, ntx)
         return [
             pltpu.make_async_remote_copy(
-                src_ref=home_ref.at[16, strip],
-                dst_ref=left_ref.at[q, strip],
-                send_sem=edge_send.at[0, strip],
-                recv_sem=left_recv.at[q, strip],
+                src_ref=home_ref.at[16, kind],
+                dst_ref=left_ref.at[q, kind],
+                send_sem=edge_send.at[0, kind],
+                recv_sem=left_recv.at[q, kind],
                 device_id={"ty": ty, "tx": after, "pat": turned(after, 0)},
                 device_id_type=MESH,
             ),
             pltpu.make_async_remote_copy(
-                src_ref=home_ref.at[0, strip],
-                dst_ref=right_ref.at[q, strip],
-                send_sem=edge_send.at[1, strip],
-                recv_sem=right_recv.at[q, strip],
+                src_ref=home_ref.at[0, kind],
+                dst_ref=right_ref.at[q, kind],
+                send_sem=edge_send.at[1, kind],
+                recv_sem=right_recv.at[q, kind],
                 device_id={"ty": ty, "tx": before, "pat": turned(before, npat - 1)},
                 device_id_type=MESH,
             ),
         ]
 
+    hops = (1, 3, 2)
+    for copy in loads[2:]:
+        copy.wait()
     make_strip(1)
     pl.semaphore_wait(barrier, len(greet))
-    for copy in row_copies + halo_copies(0, side_halo):
-        copy.start()
-    for copy in strip_copies(1) + edge_copies(1):
+    for copy in halo_copies(0, side_halo) + [strip_copy(1, d) for d in hops] + edge_copies(1):
         copy.start()
     for copy in halo_copies(0, row_halo[0] + row_halo[3]):
         copy.start()
+    make_strip(0)
+    for copy in [strip_copy(0, d) for d in hops] + edge_copies(0):
+        copy.start()
+    data_in[q] = home_ref[pl.ds(4 * mine, 5)]
+
+    def arrived(ref, sem):
+        pltpu.make_async_copy(ref, ref, sem).wait()
+
+    def receive(kind, d):
+        source = lax.rem(q - d + npat, npat)
+        if d:
+            strip_copy(kind, d).wait_recv()
+        keep = lane_iota((64, LANES)) % 16 < 4
+
+        @pl.when(mine == 0)
+        def _():
+            arrived(left_ref.at[source, kind], left_recv.at[source, kind])
+            data_in[source, 0, kind] = jnp.where(
+                keep, left_ref[source, kind], data_in[source, 0, kind]
+            )
+
+        @pl.when(mine == npat - 1)
+        def _():
+            arrived(right_ref.at[source, kind], right_recv.at[source, kind])
+            data_in[source, 4, kind] = jnp.where(
+                keep, data_in[source, 4, kind], right_ref[source, kind]
+            )
+
+    lower = lane_iota((64, LANES)) < 64
+
+    def relay_copies(d):
+        source = lax.rem(q - d + npat, npat)
+        return [
+            pltpu.make_async_remote_copy(
+                src_ref=relay_out.at[way, d],
+                dst_ref=relay_in.at[way, source],
+                send_sem=relay_send.at[way, d],
+                recv_sem=relay_recv.at[way, d],
+                device_id=at(1 - 2 * way, 0),
+                device_id_type=MESH,
+            )
+            for way in range(2)
+        ]
+
+    def relay(d):
+        source = lax.rem(q - d + npat, npat)
+        receive(1, d)
+        for k in range(2):
+            a, b = data_in[source, 2 * k, 1], data_in[source, 2 * k + 1, 1]
+            relay_out[0, d, k] = jnp.where(lower, a, pltpu.roll(b, 64, 1))
+            relay_out[1, d, k] = jnp.where(lower, pltpu.roll(a, 64, 1), b)
+        for way in range(2):
+            relay_out[way, d, 2] = data_in[source, 4, 1]
+        for copy in relay_copies(d):
+            copy.start()
+
+    def outer_strips(d):
+        source = lax.rem(q - d + npat, npat)
+        for copy in relay_copies(d):
+            copy.wait_recv()
+        for chunk in range(5):
+            own = data_in[source, chunk, 1]
+            above, below = relay_in[0, source, chunk // 2], relay_in[1, source, chunk // 2]
+            if chunk % 2:
+                above = pltpu.roll(above, 64, 1)
+            elif chunk < 4:
+                below = pltpu.roll(below, 64, 1)
+            data_mid[source, chunk, 0] = jnp.where(lower, above, own)
+            data_mid[source, chunk, 1] = jnp.where(lower, own, below)
 
     taps = [
         [jnp.where(abs(j - 4) <= radius_ref[i], taps_ref[i, j], 0.0) for j in range(TAPS)]
@@ -312,13 +375,7 @@
     full = lax.dot_general(left_adj.astype(jnp.bfloat16), spread, nt, preferred_element_type=jnp.float32)
     axial_adj[...] = jnp.where(same, full, 0.0).astype(jnp.bfloat16)
 
-    for copy in row_copies:
-        copy.wait_recv()
-    for strip in (2, 0):
-        make_strip(strip)
-        for copy in strip_copies(strip) + edge_copies(strip):
-            copy.start()
-    data_tiles[q] = home_ref[pl.ds(4 * mine, 5)]
+    relay(0)
 
     plane = row_iota((32, LANES)).astype(jnp.float32)
     planes_ref[...] = jnp.cos(plane * (2.0 * math.pi * 3.0 / 32.0))
@@ -394,18 +451,22 @@
         x, y = 16 * chunk + own_col, 8 * strip + own_row
         return (x >= 4) & (x < 68) & (y >= 4) & (y < 20)
 
-    def predict(strip, chunk):
-        tile = 4 * chunk + strip
-        if chunk == 4:
-            return jnp.dot(
-                blur_ref[:, LANES * tile : LANES * (tile + 2)],
-                forward_ref[0:256, 0:LANES],
-                preferred_element_type=jnp.float32,
-            )
+    blocks = ((1, 2), (0, 1), (3, 2))
+
+    def predict(strip, chunk, width):
+        count = min(width + 1, 5 - chunk)
         window = jnp.concatenate(
-            [blur_ref[:, LANES * (tile + 4 * k) : LANES * (tile + 4 * k + 2)] for k in range(3)], axis=1
+            [
+                blur_ref[:, LANES * (4 * (chunk + k) + strip) : LANES * (4 * (chunk + k) + strip + 2)]
+                for k in range(count)
+            ],
+            axis=1,
         )
-        return jnp.dot(window, forward_ref[...], preferred_element_type=jnp.float32)
+        return jnp.dot(
+            window,
+            forward_ref[0 : 256 * count, 0 : LANES * width],
+            preferred_element_type=jnp.float32,
+        )
 
     def compare(strip, chunk, predicted, squares):
         for k in range(predicted.shape[1] // LANES):
@@ -414,7 +475,10 @@
             filler = 1.0 - ok
             total = jnp.zeros((8, LANES), jnp.float32)
             for source in range(4):
-                data = data_tiles[source, chunk + k, strip]
+                if strip == 1:
+                    data = data_in[source, chunk + k, 0]
+                else:
+                    data = data_mid[source, chunk + k, strip // 2]
                 guess = predicted[64 * source : 64 * (source + 1), LANES * k : LANES * (k + 1)]
                 misfit = data - guess
                 total = total + jnp.sum((misfit * misfit).reshape(8, 8, LANES), axis=0)
@@ -459,10 +523,10 @@
             total = total + slots[k]
         return total
 
-    def lit_tiles(t, strips):
+    def lit_tiles(t, strips, chunks=range(5)):
         wave_z = planes_ref[...]
         left_half = lane_iota((32, LANES)) % 16 < 8
-        for chunk in range(5):
+        for chunk in chunks:
             for strip in strips:
                 tile = 4 * chunk + strip
                 a, b = grid_ref[t, chunk, strip], grid_ref[t, chunk + 1, strip]
@@ -473,7 +537,7 @@
                     lit_ref[32 * p : 32 * (p + 1), LANES * tile : LANES * (tile + 1)] = (
                         light * value
                     ).astype(jnp.bfloat16)
-        tiles = [4 * chunk + strip for chunk in range(5) for strip in strips]
+        tiles = [4 * chunk + strip for chunk in chunks for strip in strips]
         for k in range(0, len(tiles), 2):
             pair = [slice(LANES * tile, LANES * (tile + 1)) for tile in tiles[k : k + 2]]
             lit = jnp.concatenate([lit_ref[:, lanes] for lanes in pair], axis=1)
@@ -484,30 +548,6 @@
     def wait_halo(t, which):
         for copy in halo_copies(t, which):
             copy.wait_recv()
-
-    def wait_data(strip):
-        for copy in strip_copies(strip):
-            copy.wait_recv()
-        keep = lane_iota((64, LANES)) % 16 < 4
-
-        @pl.when(mine == 0)
-        def _():
-            for source in range(4):
-                arrived(left_ref.at[source, strip], left_recv.at[source, strip])
-                data_tiles[source, 0, strip] = jnp.where(
-                    keep, left_ref[source, strip], data_tiles[source, 0, strip]
-                )
-
-        @pl.when(mine == npat - 1)
-        def _():
-            for source in range(4):
-                arrived(right_ref.at[source, strip], right_recv.at[source, strip])
-                data_tiles[source, 4, strip] = jnp.where(
-                    keep, data_tiles[source, 4, strip], right_ref[source, strip]
-                )
-
-    def arrived(ref, sem):
-        pltpu.make_async_copy(ref, ref, sem).wait()
 
     def back_project(t, strip):
         wave_z = planes_ref[...]
@@ -547,14 +587,13 @@
             for d in range(1, npat)
         ]
 
-    def compare_strip(t, strip, squares):
-        for chunk in (0, 2, 4):
+    def compare_strip(t, strip, squares, some=blocks):
+        for chunk, width in some:
             if t == 0:
-                width = LANES if chunk == 4 else 2 * LANES
                 tile = 5 * strip + chunk
-                predicted = pred_ref[:, LANES * tile : LANES * tile + width]
+                predicted = pred_ref[:, LANES * tile : LANES * (tile + width)]
             else:
-                predicted = predict(strip, chunk)
+                predicted = predict(strip, chunk, width)
             squares = compare(strip, chunk, predicted, squares)
         return squares
 
@@ -576,31 +615,40 @@
         near, far = (2, 0) if early == 1 else (0, 2)
         near_halo, far_halo = (3, 0) if early == 1 else (0, 3)
         squares = jnp.zeros((8, LANES), jnp.float32)
-        wait_halo(t, side_halo)
-        lit_tiles(t, (1, 2))
+        lit_tiles(t, (1, 2), (1, 2, 3))
         if t == 0:
+            wait_halo(t, side_halo)
+            lit_tiles(t, (1, 2), (0, 4))
             wait_halo(t, row_halo[0] + row_halo[3])
             lit_tiles(t, (0, 3))
             for strip in range(3):
-                for chunk in (0, 2, 4):
-                    width = LANES if chunk == 4 else 2 * LANES
+                for chunk, width in blocks:
                     tile = 5 * strip + chunk
-                    pred_ref[:, LANES * tile : LANES * tile + width] = predict(strip, chunk)
-            wait_data(1)
-        squares = compare_strip(t, 1, squares)
-        if t == 0:
-            wait_data(near)
+                    pred_ref[:, LANES * tile : LANES * (tile + width)] = predict(
+                        strip, chunk, width
+                    )
+            for d in hops:
+                relay(d)
+            for d in (0, *hops):
+                outer_strips(d)
+            squares = compare_strip(t, near, squares)
+            squares = compare_strip(t, far, squares)
+            for d in (0, *hops):
+                receive(0, d)
+            squares = compare_strip(t, 1, squares)
+            finish_strip(t, early)
         else:
+            squares = compare_strip(t, 1, squares, blocks[:1])
+            wait_halo(t, side_halo)
+            lit_tiles(t, (1, 2), (0, 4))
+            squares = compare_strip(t, 1, squares, blocks[1:])
             wait_halo(t, row_halo[near_halo])
             lit_tiles(t, (near_halo,))
-        squares = compare_strip(t, near, squares)
-        finish_strip(t, early)
-        if t == 0:
-            wait_data(far)
-        else:
+            squares = compare_strip(t, near, squares)
+            finish_strip(t, early)
             wait_halo(t, row_halo[far_halo])
             lit_tiles(t, (far_halo,))
-        squares = compare_strip(t, far, squares)
+            squares = compare_strip(t, far, squares)
         squares_ref[t] = squares
         if t == ITERS - 1:
             share = jnp.zeros((8, LANES), jnp.float32)
@@ -611,10 +659,11 @@
         finish_strip(t, 1 - early)
 
     send_sums(1, gather_sums(0))
-    for copy in row_copies:
-        copy.wait_send()
-    for strip in range(3):
-        for copy in strip_copies(strip) + edge_copies(strip):
+    for kind in range(2):
+        for copy in [strip_copy(kind, d) for d in hops] + edge_copies(kind):
+            copy.wait_send()
+    for d in range(npat):
+        for copy in relay_copies(d):
             copy.wait_send()
     for t in range(ITERS):
         for copy in halo_copies(t, range(len(moves))):
@@ -625,9 +674,19 @@
         for half in range(2):
             tiles = [final_ref[2 * half + k // 4, k % 4, strip] for k in range(8)]
             for y, row in enumerate(block_transpose(tiles)):
-                out_ref[8 * strip + y, :, LANES * half : LANES * (half + 1)] = row
+                out_rows[half, pl.ds(8 * strip + y, 32, stride=16)] = row
+    stores = [
+        pltpu.make_async_copy(
+            out_rows.at[half], out_ref.at[:, LANES * half : LANES * (half + 1)], store_sem.at[half]
+        )
+        for half in range(2)
+    ]
+    for copy in stores:
+        copy.start()
     total = jnp.sum(gather_sums(1), axis=1, keepdims=True)
     rms_ref[...] = jnp.broadcast_to(jnp.sqrt(total / cells), (8, LANES))
+    for copy in stores:
+        copy.wait()
 
 
 def per_device(estimate, data, axial, lateral_kernel, psf_radius, pattern_codes):
@@ -635,9 +694,10 @@
     local = data.shape[0]
     full_rows = height * lax.axis_size("ty")
     full_cols = width * lax.axis_size("tx")
-    est_rows = estimate.transpose(1, 0, 2)
-    data_rows = data.transpose(2, 0, 1, 3).reshape(height, local * planes, width)
+    est_rows = estimate.reshape(planes * height, width)
+    data_rows = data.reshape(local * planes * height, width)
     vmem = pl.BlockSpec(memory_space=pltpu.VMEM)
+    hbm = pl.BlockSpec(memory_space=pltpu.HBM)
     smem = pl.BlockSpec(memory_space=pltpu.SMEM)
     f32, bf16 = jnp.float32, jnp.bfloat16
     dma = pltpu.SemaphoreType.DMA
@@ -646,23 +706,29 @@
         functools.partial(kernel, full_rows, full_cols, cells),
         name="deconvolve",
         out_shape=(
-            jax.ShapeDtypeStruct((height, planes, width), f32),
+            jax.ShapeDtypeStruct((planes * height, width), f32),
             jax.ShapeDtypeStruct((8, LANES), f32),
         ),
-        in_specs=[vmem, vmem, vmem, smem, smem, smem],
-        out_specs=(vmem, vmem),
+        in_specs=[hbm, hbm, vmem, smem, smem, smem],
+        out_specs=(hbm, vmem),
         scratch_shapes=[
             pltpu.VMEM((ITERS, 8, LANES), f32),
             pltpu.VMEM((lax.axis_size(("tx", "pat")), 8, LANES), f32),
             pltpu.VMEM((lax.axis_size("ty"), 8, LANES), f32),
+            pltpu.VMEM((2, planes * height, LANES), f32),
+            pltpu.VMEM((2, local * planes * height, LANES), f32),
+            pltpu.VMEM((2, planes * height, LANES), f32),
+            dma((2, 2)),
+            dma((2,)),
             pltpu.VMEM((ITERS, 6, 4, 32, LANES), f32),
             pltpu.VMEM((4, 4, 2, 32, LANES), f32),
-            pltpu.VMEM((17, 3, 64, LANES), f32),
-            pltpu.VMEM((4, 5, 3, 64, LANES), f32),
-            pltpu.VMEM((4, 64, 256), f32),
-            pltpu.VMEM((4, 64, 256), f32),
-            pltpu.VMEM((4, 3, 64, LANES), f32),
-            pltpu.VMEM((4, 3, 64, LANES), f32),
+            pltpu.VMEM((17, 2, 64, LANES), f32),
+            pltpu.VMEM((4, 5, 2, 64, LANES), f32),
+            pltpu.VMEM((4, 5, 2, 64, LANES), f32),
+            pltpu.VMEM((2, 4, 3, 64, LANES), f32),
+            pltpu.VMEM((2, 4, 3, 64, LANES), f32),
+            pltpu.VMEM((4, 2, 64, LANES), f32),
+            pltpu.VMEM((4, 2, 64, LANES), f32),
             pltpu.VMEM((256, 20 * LANES), bf16),
             pltpu.VMEM((256, 20 * LANES), bf16),
             pltpu.VMEM((256, 15 * LANES), f32),
@@ -679,13 +745,13 @@
             pltpu.VMEM((8, 32, LANES), f32),
             dma((ITERS, 10)),
             dma((ITERS, 10)),
-            dma((2,)),
-            dma((2,)),
+            dma((2, 4)),
+            dma((2, 4)),
+            dma((2, 2)),
+            dma((4, 2)),
+            dma((4, 2)),
             dma((2, 3)),
-            dma((4, 3)),
-            dma((4, 3)),
-            dma((3, 3)),
-            dma((3, 3)),
+            dma((2, 3)),
             dma((2, 3)),
             dma((2, 3)),
             dma((2, 15)),
@@ -695,7 +761,7 @@
             collective_id=0, has_side_effects=True, vmem_limit_bytes=56 * 1024 * 1024
         ),
     )(est_rows, data_rows, axial, lateral_kernel, psf_radius, pattern_codes)
-    return rows.transpose(1, 0, 2), rms[:ITERS, 0]
+    return rows.reshape(planes, height, width), rms[:ITERS, 0]
 
 
 def solution(mesh):

time: 81 us -> 71.4 us (0.88)
  Pallas kernels: 73.6 us -> 67.3 us
  local copies, waits for them, and re-layouts: 6.6 us -> 3.17 us
    pallas_call x1, Pallas kernels: 73.6 us -> 67.3 us  [per_device(): pl.pallas_call(functools.partial(kernel, full_rows, full_cols, cells), na...]
    unnamed x6 -> x3, local copies, waits for them, and re-layouts: 4.38 us -> 2.54 us
    transpose x1 -> x0, local copies, waits for them, and re-layouts: 1.6 us -> none  [per_device(): data.transpose(2, 0, 1, 3).reshape(height, local * planes, width)]
where the time goes in v3:
time: 71.4 us; the launch traced here: 71.1 us
  Pallas kernels  67.3 us (94%)
  local copies, waits for them, and re-layouts  3.17 us (4%)
    pallas_call x1, Pallas kernels, per_device(): pl.pallas_call(functools.partial(kernel, full_rows, full_cols, cells), na...  67.3 us
    unnamed x3, local copies, waits for them, and re-layouts  2.54 us

profile of v3, /device:TPU:1, one launch (start us, length us, event | category | flops | bytes accessed | tf_op | source)
XLA Modules:
  0.0 71.1 jit_solution(7068020222691572730)
XLA Ops:
  0.6 67.3 %deconvolve.1 = (f32[512,256]{1,0:T(8,128)}, f32[8,128]{1,0:T(8,128)}) custom-call(f32[512,256]{1,0:T(8,128)} %bitcast.4, f32[1024,256]{1,0:T(8,128)} %bitcast.3, f32[32,32]{1,0:T(8,128)} %axial_ref.1, f32[9,9]{1,0:T(8,128)} %taps_ref.1, s32[9]{0:T(128)} %radius_ref.1, s32[2,8]{1,0:T(2,128)} %codes_ref.1), custom_call_target="tpu_custom_call" | custom-call | tf_op jit(solution)/shard_map/deconvolve/pallas_call | solution.py:705
  67.9 0.0 copy-start
  68.0 0.7 copy-done
  68.6 0.6 slice_reduce_fusion
  69.3 1.9 %copy.9 = f32[32,16,256]{2,1,0:T(8,128)} copy(f32[32,16,256]{2,1,0:T(8,128)} %bitcast.5) | data formatting | bytes 1048576
Async XLA Ops:
  67.9 0.7 copy-start

commit v4 on v3

--- a/solution.py
+++ b/solution.py
@@ -247,9 +247,9 @@
         copy.wait()
     make_strip(1)
     pl.semaphore_wait(barrier, len(greet))
-    for copy in halo_copies(0, side_halo) + [strip_copy(1, d) for d in hops] + edge_copies(1):
+    for copy in halo_copies(0, side_halo + row_halo[0] + row_halo[3]):
         copy.start()
-    for copy in halo_copies(0, row_halo[0] + row_halo[3]):
+    for copy in [strip_copy(1, d) for d in hops] + edge_copies(1):
         copy.start()
     make_strip(0)
     for copy in [strip_copy(0, d) for d in hops] + edge_copies(0):
@@ -468,25 +468,41 @@
             preferred_element_type=jnp.float32,
         )
 
+    def compare_rows(strip, tile_chunk, source, guess):
+        tile = 3 * tile_chunk + strip
+        ok = valid_ref[tile : tile + 1, :]
+        if strip == 1:
+            data = data_in[source, tile_chunk, 0]
+        else:
+            data = data_mid[source, tile_chunk, strip // 2]
+        misfit = data - guess
+        quotient = (data * ok) / (guess + (1.0 - ok))
+        return jnp.sum((misfit * misfit).reshape(8, 8, LANES), axis=0), quotient.astype(jnp.bfloat16)
+
     def compare(strip, chunk, predicted, squares):
         for k in range(predicted.shape[1] // LANES):
             tile = 3 * (chunk + k) + strip
-            ok = valid_ref[tile : tile + 1, :]
-            filler = 1.0 - ok
             total = jnp.zeros((8, LANES), jnp.float32)
             for source in range(4):
-                if strip == 1:
-                    data = data_in[source, chunk + k, 0]
-                else:
-                    data = data_mid[source, chunk + k, strip // 2]
-                guess = predicted[64 * source : 64 * (source + 1), LANES * k : LANES * (k + 1)]
-                misfit = data - guess
-                total = total + jnp.sum((misfit * misfit).reshape(8, 8, LANES), axis=0)
-                quotient = (data * ok) / (guess + filler)
-                quot_ref[64 * source : 64 * (source + 1), LANES * tile : LANES * (tile + 1)] = (
-                    quotient.astype(jnp.bfloat16)
+                rows = slice(64 * source, 64 * (source + 1))
+                part, quotient = compare_rows(
+                    strip, chunk + k, source, predicted[rows, LANES * k : LANES * (k + 1)]
                 )
+                quot_ref[rows, LANES * tile : LANES * (tile + 1)] = quotient
+                total = total + part
             squares = squares + jnp.where(inner_mask(tile), total, 0.0)
+        return squares
+
+    def compare_source(source, squares):
+        rows = pl.ds(pl.multiple_of(64 * source, 64), 64)
+        for strip in range(3):
+            for chunk in range(5):
+                tile, place = 3 * chunk + strip, 5 * strip + chunk
+                part, quotient = compare_rows(
+                    strip, chunk, source, pred_ref[rows, LANES * place : LANES * (place + 1)]
+                )
+                quot_ref[rows, LANES * tile : LANES * (tile + 1)] = quotient
+                squares = squares + jnp.where(inner_mask(tile), part, 0.0)
         return squares
 
     stages = [
@@ -526,24 +542,33 @@
     def lit_tiles(t, strips, chunks=range(5)):
         wave_z = planes_ref[...]
         left_half = lane_iota((32, LANES)) % 16 < 8
-        for chunk in chunks:
-            for strip in strips:
-                tile = 4 * chunk + strip
-                a, b = grid_ref[t, chunk, strip], grid_ref[t, chunk + 1, strip]
-                value = jnp.where(left_half, pltpu.roll(a, LANES - 8, 1), pltpu.roll(b, 8, 1))
-                value = value * mask_ext[tile : tile + 1, :]
-                for p in range(NPAT):
-                    light = 1.0 + wave_ext[NPAT * tile + p : NPAT * tile + p + 1, :] * wave_z
-                    lit_ref[32 * p : 32 * (p + 1), LANES * tile : LANES * (tile + 1)] = (
-                        light * value
-                    ).astype(jnp.bfloat16)
-        tiles = [4 * chunk + strip for chunk in chunks for strip in strips]
-        for k in range(0, len(tiles), 2):
-            pair = [slice(LANES * tile, LANES * (tile + 1)) for tile in tiles[k : k + 2]]
+
+        def light(tile):
+            chunk, strip = tile // 4, tile % 4
+            a, b = grid_ref[t, chunk, strip], grid_ref[t, chunk + 1, strip]
+            value = jnp.where(left_half, pltpu.roll(a, LANES - 8, 1), pltpu.roll(b, 8, 1))
+            value = value * mask_ext[tile : tile + 1, :]
+            for p in range(NPAT):
+                wave = 1.0 + wave_ext[NPAT * tile + p : NPAT * tile + p + 1, :] * wave_z
+                lit_ref[32 * p : 32 * (p + 1), LANES * tile : LANES * (tile + 1)] = (
+                    wave * value
+                ).astype(jnp.bfloat16)
+
+        def blur(pair):
+            pair = [slice(LANES * tile, LANES * (tile + 1)) for tile in pair]
             lit = jnp.concatenate([lit_ref[:, lanes] for lanes in pair], axis=1)
             blurred = jnp.dot(axial_fwd[...], lit, preferred_element_type=jnp.float32)
             for n, lanes in enumerate(pair):
                 blur_ref[:, lanes] = blurred[:, LANES * n : LANES * (n + 1)].astype(jnp.bfloat16)
+
+        tiles = [4 * chunk + strip for chunk in chunks for strip in strips]
+        pairs = [tiles[k : k + 2] for k in range(0, len(tiles), 2)]
+        for k, pair in enumerate(pairs):
+            for tile in pair:
+                light(tile)
+            if k:
+                blur(pairs[k - 1])
+        blur(pairs[-1])
 
     def wait_halo(t, which):
         for copy in halo_copies(t, which):
@@ -587,15 +612,14 @@
             for d in range(1, npat)
         ]
 
-    def compare_strip(t, strip, squares, some=blocks):
+    def compare_strip(strip, squares, some=blocks):
+        waiting = None
         for chunk, width in some:
-            if t == 0:
-                tile = 5 * strip + chunk
-                predicted = pred_ref[:, LANES * tile : LANES * (tile + width)]
-            else:
-                predicted = predict(strip, chunk, width)
-            squares = compare(strip, chunk, predicted, squares)
-        return squares
+            predicted = predict(strip, chunk, width)
+            if waiting is not None:
+                squares = compare(strip, *waiting, squares)
+            waiting = chunk, predicted
+        return compare(strip, *waiting, squares)
 
     def finish_strip(t, strip):
         for chunk, value in back_project(t, strip):
@@ -631,24 +655,24 @@
                 relay(d)
             for d in (0, *hops):
                 outer_strips(d)
-            squares = compare_strip(t, near, squares)
-            squares = compare_strip(t, far, squares)
-            for d in (0, *hops):
                 receive(0, d)
-            squares = compare_strip(t, 1, squares)
+                squares = compare_source(lax.rem(q - d + npat, npat), squares)
             finish_strip(t, early)
         else:
-            squares = compare_strip(t, 1, squares, blocks[:1])
+            squares = compare_strip(1, squares, blocks[:1])
+            wait_halo(t, row_halo[near_halo][:1])
+            lit_tiles(t, (near_halo,), (1, 2, 3))
+            squares = compare_strip(near, squares, blocks[:1])
             wait_halo(t, side_halo)
             lit_tiles(t, (1, 2), (0, 4))
-            squares = compare_strip(t, 1, squares, blocks[1:])
-            wait_halo(t, row_halo[near_halo])
-            lit_tiles(t, (near_halo,))
-            squares = compare_strip(t, near, squares)
+            squares = compare_strip(1, squares, blocks[1:])
+            wait_halo(t, row_halo[near_halo][1:])
+            lit_tiles(t, (near_halo,), (0, 4))
+            squares = compare_strip(near, squares, blocks[1:])
             finish_strip(t, early)
             wait_halo(t, row_halo[far_halo])
             lit_tiles(t, (far_halo,))
-            squares = compare_strip(t, far, squares)
+            squares = compare_strip(far, squares)
         squares_ref[t] = squares
         if t == ITERS - 1:
             share = jnp.zeros((8, LANES), jnp.float32)

time: 71.4 us -> 69.4 us (0.972)
  Pallas kernels: 67.3 us -> 65.4 us
    pallas_call x1, Pallas kernels: 67.3 us -> 65.4 us  [per_device(): pl.pallas_call(functools.partial(kernel, full_rows, full_cols, cells), na...]
where the time goes in v4:
time: 69.4 us; the launch traced here: 69.2 us
  Pallas kernels  65.4 us (94%)
  local copies, waits for them, and re-layouts  3.17 us (5%)
    pallas_call x1, Pallas kernels, per_device(): pl.pallas_call(functools.partial(kernel, full_rows, full_cols, cells), na...  65.4 us
    unnamed x3, local copies, waits for them, and re-layouts  2.54 us

profile of v4, /device:TPU:1, one launch (start us, length us, event | category | flops | bytes accessed | tf_op | source)
XLA Modules:
  0.0 69.2 jit_solution(13852787219785937938)
XLA Ops:
  0.6 65.4 %deconvolve.1 = (f32[512,256]{1,0:T(8,128)}, f32[8,128]{1,0:T(8,128)}) custom-call(f32[512,256]{1,0:T(8,128)} %bitcast.4, f32[1024,256]{1,0:T(8,128)} %bitcast.3, f32[32,32]{1,0:T(8,128)} %axial_ref.1, f32[9,9]{1,0:T(8,128)} %taps_ref.1, s32[9]{0:T(128)} %radius_ref.1, s32[2,8]{1,0:T(2,128)} %codes_ref.1), custom_call_target="tpu_custom_call" | custom-call | tf_op jit(solution)/shard_map/deconvolve/pallas_call | solution.py:729
  66.0 0.0 copy-start
  66.0 0.7 copy-done
  66.7 0.6 slice_reduce_fusion
  67.3 1.9 %copy.9 = f32[32,16,256]{2,1,0:T(8,128)} copy(f32[32,16,256]{2,1,0:T(8,128)} %bitcast.5) | data formatting | bytes 1048576
Async XLA Ops:
  66.0 0.7 copy-start

commit v5 on v4

--- a/solution.py
+++ b/solution.py
@@ -154,8 +154,10 @@
     grid_ref[0, 1:5, 1:3] = final_ref[mine]
 
     moves = [
-        ((slice(1, 5), 1), (slice(1, 5), 3), -1, 0),
-        ((slice(1, 5), 2), (slice(1, 5), 0), 1, 0),
+        ((slice(1, 3), 1), (slice(1, 3), 3), -1, 0),
+        ((slice(3, 5), 1), (slice(3, 5), 3), -1, 0),
+        ((slice(1, 3), 2), (slice(1, 3), 0), 1, 0),
+        ((slice(3, 5), 2), (slice(3, 5), 0), 1, 0),
         ((1, 1), (5, 1), 0, -1),
         ((4, 1), (0, 1), 0, 1),
         ((1, 2), (5, 2), 0, -1),
@@ -165,9 +167,11 @@
         ((1, 2), (5, 0), 1, -1),
         ((4, 2), (0, 0), 1, 1),
     ]
-    from_strip = ((2, 3, 0, 6, 7), (4, 5, 1, 8, 9))
-    side_halo = (2, 3, 4, 5)
-    row_halo = {0: (1, 8, 9), 3: (0, 6, 7)}
+    from_strip = (((8, 4, 0), (9, 5, 1)), ((10, 6, 2), (11, 7, 3)))
+    side_halo = (4, 5, 6, 7)
+    row_halo = {0: (2, 3), 3: (0, 1)}
+    corner_halo = {0: (10, 11), 3: (8, 9)}
+    all_halo = (8, 9, 10, 11, 4, 5, 6, 7, 0, 1, 2, 3)
 
     def halo_copies(t, which):
         copies = []
@@ -247,7 +251,7 @@
         copy.wait()
     make_strip(1)
     pl.semaphore_wait(barrier, len(greet))
-    for copy in halo_copies(0, side_halo + row_halo[0] + row_halo[3]):
+    for copy in halo_copies(0, all_halo):
         copy.start()
     for copy in [strip_copy(1, d) for d in hops] + edge_copies(1):
         copy.start()
@@ -574,29 +578,28 @@
         for copy in halo_copies(t, which):
             copy.wait_recv()
 
-    def back_project(t, strip):
+    def back_project(t, strip, chunk):
         wave_z = planes_ref[...]
         updated = []
-        for chunk in (0, 2):
-            tile = 3 * chunk + strip
-            window = jnp.concatenate(
-                [quot_ref[:, LANES * (tile + 3 * k) : LANES * (tile + 3 * k + 2)] for k in range(3)],
-                axis=1,
-            )
-            spread_back = jnp.dot(
-                window, adjoint_ref[...], preferred_element_type=jnp.float32
-            ).astype(jnp.bfloat16)
-            gathered = jnp.dot(axial_adj[...], spread_back, preferred_element_type=jnp.float32)
-            for k in range(2):
-                here = 2 * (chunk + k) + strip
-                summed = jnp.zeros((32, LANES), jnp.float32)
-                for p in range(NPAT):
-                    light = 1.0 + wave_in[NPAT * here + p : NPAT * here + p + 1, :] * wave_z
-                    summed = summed + light * gathered[
-                        32 * p : 32 * (p + 1), LANES * k : LANES * (k + 1)
-                    ]
-                current = grid_ref[t, 1 + chunk + k, 1 + strip]
-                updated.append((chunk + k, current * summed / norm_ref[here]))
+        tile = 3 * chunk + strip
+        window = jnp.concatenate(
+            [quot_ref[:, LANES * (tile + 3 * k) : LANES * (tile + 3 * k + 2)] for k in range(3)],
+            axis=1,
+        )
+        spread_back = jnp.dot(
+            window, adjoint_ref[...], preferred_element_type=jnp.float32
+        ).astype(jnp.bfloat16)
+        gathered = jnp.dot(axial_adj[...], spread_back, preferred_element_type=jnp.float32)
+        for k in range(2):
+            here = 2 * (chunk + k) + strip
+            summed = jnp.zeros((32, LANES), jnp.float32)
+            for p in range(NPAT):
+                light = 1.0 + wave_in[NPAT * here + p : NPAT * here + p + 1, :] * wave_z
+                summed = summed + light * gathered[
+                    32 * p : 32 * (p + 1), LANES * k : LANES * (k + 1)
+                ]
+            current = grid_ref[t, 1 + chunk + k, 1 + strip]
+            updated.append((chunk + k, current * summed / norm_ref[here]))
         return updated
 
     def out_copies(strip):
@@ -622,17 +625,26 @@
         return compare(strip, *waiting, squares)
 
     def finish_strip(t, strip):
-        for chunk, value in back_project(t, strip):
-            if t == ITERS - 1:
-                final_ref[mine, chunk, strip] = value
-            else:
-                grid_ref[t + 1, 1 + chunk, 1 + strip] = value
-        if t == ITERS - 1:
-            copies = out_copies(strip)
-        else:
-            copies = halo_copies(t + 1, from_strip[strip])
-        for copy in copies:
-            copy.start()
+        last = t == ITERS - 1
+        for block in range(2):
+            for chunk, value in back_project(t, strip, 2 * block):
+                if last:
+                    final_ref[mine, chunk, strip] = value
+                else:
+                    grid_ref[t + 1, 1 + chunk, 1 + strip] = value
+            if not last:
+                for copy in halo_copies(t + 1, from_strip[strip][block]):
+                    copy.start()
+        if last:
+            for copy in out_copies(strip):
+                copy.start()
+
+    def share_squares():
+        share = jnp.zeros((8, LANES), jnp.float32)
+        for k in range(ITERS):
+            total = jnp.sum(squares_ref[k], axis=0, keepdims=True)
+            share = jnp.where(row_iota((8, LANES)) == k, total, share)
+        send_sums(0, share)
 
     for t in range(ITERS):
         early = 1 - t % 2
@@ -643,7 +655,7 @@
         if t == 0:
             wait_halo(t, side_halo)
             lit_tiles(t, (1, 2), (0, 4))
-            wait_halo(t, row_halo[0] + row_halo[3])
+            wait_halo(t, all_halo[:4] + all_halo[8:])
             lit_tiles(t, (0, 3))
             for strip in range(3):
                 for chunk, width in blocks:
@@ -657,29 +669,30 @@
                 outer_strips(d)
                 receive(0, d)
                 squares = compare_source(lax.rem(q - d + npat, npat), squares)
-            finish_strip(t, early)
         else:
             squares = compare_strip(1, squares, blocks[:1])
-            wait_halo(t, row_halo[near_halo][:1])
+            wait_halo(t, row_halo[near_halo])
             lit_tiles(t, (near_halo,), (1, 2, 3))
             squares = compare_strip(near, squares, blocks[:1])
             wait_halo(t, side_halo)
             lit_tiles(t, (1, 2), (0, 4))
             squares = compare_strip(1, squares, blocks[1:])
-            wait_halo(t, row_halo[near_halo][1:])
+            wait_halo(t, corner_halo[near_halo])
             lit_tiles(t, (near_halo,), (0, 4))
             squares = compare_strip(near, squares, blocks[1:])
-            finish_strip(t, early)
+            if t < ITERS - 1:
+                finish_strip(t, early)
             wait_halo(t, row_halo[far_halo])
-            lit_tiles(t, (far_halo,))
-            squares = compare_strip(far, squares)
+            lit_tiles(t, (far_halo,), (1, 2, 3))
+            squares = compare_strip(far, squares, blocks[:1])
+            wait_halo(t, corner_halo[far_halo])
+            lit_tiles(t, (far_halo,), (0, 4))
+            squares = compare_strip(far, squares, blocks[1:])
         squares_ref[t] = squares
         if t == ITERS - 1:
-            share = jnp.zeros((8, LANES), jnp.float32)
-            for k in range(ITERS):
-                total = jnp.sum(squares_ref[k], axis=0, keepdims=True)
-                share = jnp.where(row_iota((8, LANES)) == k, total, share)
-            send_sums(0, share)
+            share_squares()
+        if t == 0 or t == ITERS - 1:
+            finish_strip(t, early)
         finish_strip(t, 1 - early)
 
     send_sums(1, gather_sums(0))
@@ -690,7 +703,7 @@
         for copy in relay_copies(d):
             copy.wait_send()
     for t in range(ITERS):
-        for copy in halo_copies(t, range(len(moves))):
+        for copy in halo_copies(t, all_halo):
             copy.wait_send()
     for strip in (early, 1 - early):
         for copy in out_copies(strip):
@@ -708,7 +721,9 @@
     for copy in stores:
         copy.start()
     total = jnp.sum(gather_sums(1), axis=1, keepdims=True)
-    rms_ref[...] = jnp.broadcast_to(jnp.sqrt(total / cells), (8, LANES))
+    rms = jnp.sqrt(total / cells)
+    for k in range(ITERS):
+        rms_ref[k] = rms[k, 0]
     for copy in stores:
         copy.wait()
 
@@ -731,10 +746,10 @@
         name="deconvolve",
         out_shape=(
             jax.ShapeDtypeStruct((planes * height, width), f32),
-            jax.ShapeDtypeStruct((8, LANES), f32),
+            jax.ShapeDtypeStruct((ITERS,), f32),
         ),
         in_specs=[hbm, hbm, vmem, smem, smem, smem],
-        out_specs=(hbm, vmem),
+        out_specs=(hbm, smem),
         scratch_shapes=[
             pltpu.VMEM((ITERS, 8, LANES), f32),
             pltpu.VMEM((lax.axis_size(("tx", "pat")), 8, LANES), f32),
@@ -767,8 +782,8 @@
             pltpu.VMEM((24, LANES), f32),
             pltpu.VMEM((16, LANES), f32),
             pltpu.VMEM((8, 32, LANES), f32),
-            dma((ITERS, 10)),
-            dma((ITERS, 10)),
+            dma((ITERS, 12)),
+            dma((ITERS, 12)),
             dma((2, 4)),
             dma((2, 4)),
             dma((2, 2)),
@@ -785,7 +800,7 @@
             collective_id=0, has_side_effects=True, vmem_limit_bytes=56 * 1024 * 1024
         ),
     )(est_rows, data_rows, axial, lateral_kernel, psf_radius, pattern_codes)
-    return rows.reshape(planes, height, width), rms[:ITERS, 0]
+    return rows.reshape(planes, height, width), rms
 
 
 def solution(mesh):

time: 69.4 us -> 69.3 us (level)
  local copies, waits for them, and re-layouts: 3.17 us -> 2.38 us
  Pallas kernels: 65.4 us -> 66.1 us
    pallas_call x1, Pallas kernels: 65.4 us -> 66.1 us  [per_device(): pl.pallas_call(functools.partial(kernel, full_rows, full_cols, cells), na...]
    unnamed x3 -> x4, local copies, waits for them, and re-layouts: 2.54 us -> 2.38 us
where the time goes in v5:
time: 69.3 us; the launch traced here: 69.1 us
  Pallas kernels  66.1 us (95%)
  local copies, waits for them, and re-layouts  2.38 us (3%)
    pallas_call x1, Pallas kernels, per_device(): pl.pallas_call(functools.partial(kernel, full_rows, full_cols, cells), na...  66.1 us
    unnamed x4, local copies, waits for them, and re-layouts  2.38 us

profile of v5, /device:TPU:1, one launch (start us, length us, event | category | flops | bytes accessed | tf_op | source)
XLA Modules:
  0.0 69.1 jit_solution(12939348295515403982)
XLA Ops:
  0.6 66.1 %deconvolve.1 = (f32[512,256]{1,0:T(8,128)}, f32[4]{0:T(128)}) custom-call(f32[512,256]{1,0:T(8,128)} %bitcast.4, f32[1024,256]{1,0:T(8,128)} %bitcast.3, f32[32,32]{1,0:T(8,128)} %axial_ref.1, f32[9,9]{1,0:T(8,128)} %taps_ref.1, s32[9]{0:T(128)} %radius_ref.1, s32[2,8]{1,0:T(2,128)} %codes_ref.1), custom_call_target="tpu_custom_call" | custom-call | tf_op jit(solution)/shard_map/deconvolve/pallas_call | solution.py:744
  66.7 0.0 copy-start
  66.7 1.9 %copy.10 = f32[32,16,256]{2,1,0:T(8,128)} copy(f32[32,16,256]{2,1,0:T(8,128)} %bitcast.5) | data formatting | bytes 1048576
  68.6 0.0 copy-done
  68.6 0.5 copy.11
Async XLA Ops:
  66.7 1.9 %copy-start = (f32[4]{0:T(128)S(1)}, f32[4]{0:T(128)}, u32[]{:S(2)}) copy-start(f32[4]{0:T(128)} %get-tuple-element.9) | copy-start | bytes 52

commit v6 on v5

--- a/solution.py
+++ b/solution.py
@@ -671,23 +671,16 @@
                 squares = compare_source(lax.rem(q - d + npat, npat), squares)
         else:
             squares = compare_strip(1, squares, blocks[:1])
-            wait_halo(t, row_halo[near_halo])
-            lit_tiles(t, (near_halo,), (1, 2, 3))
-            squares = compare_strip(near, squares, blocks[:1])
-            wait_halo(t, side_halo)
+            wait_halo(t, side_halo + row_halo[near_halo] + corner_halo[near_halo])
             lit_tiles(t, (1, 2), (0, 4))
+            lit_tiles(t, (near_halo,))
             squares = compare_strip(1, squares, blocks[1:])
-            wait_halo(t, corner_halo[near_halo])
-            lit_tiles(t, (near_halo,), (0, 4))
-            squares = compare_strip(near, squares, blocks[1:])
+            squares = compare_strip(near, squares)
             if t < ITERS - 1:
                 finish_strip(t, early)
-            wait_halo(t, row_halo[far_halo])
-            lit_tiles(t, (far_halo,), (1, 2, 3))
-            squares = compare_strip(far, squares, blocks[:1])
-            wait_halo(t, corner_halo[far_halo])
-            lit_tiles(t, (far_halo,), (0, 4))
-            squares = compare_strip(far, squares, blocks[1:])
+            wait_halo(t, row_halo[far_halo] + corner_halo[far_halo])
+            lit_tiles(t, (far_halo,))
+            squares = compare_strip(far, squares)
         squares_ref[t] = squares
         if t == ITERS - 1:
             share_squares()

time: 69.3 us -> 67.3 us (0.971)
  Pallas kernels: 66.1 us -> 63.8 us
    pallas_call x1, Pallas kernels: 66.1 us -> 63.8 us  [per_device(): pl.pallas_call(functools.partial(kernel, full_rows, full_cols, cells), na...]
where the time goes in v6:
time: 67.3 us; the launch traced here: 66.8 us
  Pallas kernels  63.8 us (95%)
  local copies, waits for them, and re-layouts  2.38 us (4%)
    pallas_call x1, Pallas kernels, per_device(): pl.pallas_call(functools.partial(kernel, full_rows, full_cols, cells), na...  63.8 us
    unnamed x4, local copies, waits for them, and re-layouts  2.38 us

profile of v6, /device:TPU:1, one launch (start us, length us, event | category | flops | bytes accessed | tf_op | source)
XLA Modules:
  0.0 66.8 jit_solution(15204021921908219451)
XLA Ops:
  0.6 63.8 %deconvolve.1 = (f32[512,256]{1,0:T(8,128)}, f32[4]{0:T(128)}) custom-call(f32[512,256]{1,0:T(8,128)} %bitcast.4, f32[1024,256]{1,0:T(8,128)} %bitcast.3, f32[32,32]{1,0:T(8,128)} %axial_ref.1, f32[9,9]{1,0:T(8,128)} %taps_ref.1, s32[9]{0:T(128)} %radius_ref.1, s32[2,8]{1,0:T(2,128)} %codes_ref.1), custom_call_target="tpu_custom_call" | custom-call | tf_op jit(solution)/shard_map/deconvolve/pallas_call | solution.py:737
  64.4 0.0 copy-start
  64.4 1.9 %copy.10 = f32[32,16,256]{2,1,0:T(8,128)} copy(f32[32,16,256]{2,1,0:T(8,128)} %bitcast.5) | data formatting | bytes 1048576
  66.3 0.0 copy-done
  66.3 0.5 copy.11
Async XLA Ops:
  64.4 1.9 %copy-start = (f32[4]{0:T(128)S(1)}, f32[4]{0:T(128)}, u32[]{:S(2)}) copy-start(f32[4]{0:T(128)} %get-tuple-element.9) | copy-start | bytes 52

commit v7 on v6

--- a/solution.py
+++ b/solution.py
@@ -167,7 +167,7 @@
         ((1, 2), (5, 0), 1, -1),
         ((4, 2), (0, 0), 1, 1),
     ]
-    from_strip = (((8, 4, 0), (9, 5, 1)), ((10, 6, 2), (11, 7, 3)))
+    from_strip = (((4, 8, 0), (5, 9, 1)), ((6, 10, 2), (7, 11, 3)))
     side_halo = (4, 5, 6, 7)
     row_halo = {0: (2, 3), 3: (0, 1)}
     corner_halo = {0: (10, 11), 3: (8, 9)}

time: 67.3 us -> 67.2 us (level)
  no operation moved by 1% of the time
where the time goes in v7:
time: 67.2 us; the launch traced here: 66.8 us
  Pallas kernels  63.8 us (95%)
  local copies, waits for them, and re-layouts  2.38 us (4%)
    pallas_call x1, Pallas kernels, per_device(): pl.pallas_call(functools.partial(kernel, full_rows, full_cols, cells), na...  63.8 us
    unnamed x4, local copies, waits for them, and re-layouts  2.38 us

profile of v7, /device:TPU:1, one launch (start us, length us, event | category | flops | bytes accessed | tf_op | source)
XLA Modules:
  0.0 66.8 jit_solution(3832164698848971203)
XLA Ops:
  0.6 63.8 %deconvolve.1 = (f32[512,256]{1,0:T(8,128)}, f32[4]{0:T(128)}) custom-call(f32[512,256]{1,0:T(8,128)} %bitcast.4, f32[1024,256]{1,0:T(8,128)} %bitcast.3, f32[32,32]{1,0:T(8,128)} %axial_ref.1, f32[9,9]{1,0:T(8,128)} %taps_ref.1, s32[9]{0:T(128)} %radius_ref.1, s32[2,8]{1,0:T(2,128)} %codes_ref.1), custom_call_target="tpu_custom_call" | custom-call | tf_op jit(solution)/shard_map/deconvolve/pallas_call | solution.py:737
  64.4 0.0 copy-start
  64.4 1.9 %copy.10 = f32[32,16,256]{2,1,0:T(8,128)} copy(f32[32,16,256]{2,1,0:T(8,128)} %bitcast.5) | data formatting | bytes 1048576
  66.3 0.0 copy-done
  66.3 0.5 copy.11
Async XLA Ops:
  64.4 1.9 %copy-start = (f32[4]{0:T(128)S(1)}, f32[4]{0:T(128)}, u32[]{:S(2)}) copy-start(f32[4]{0:T(128)} %get-tuple-element.9) | copy-start | bytes 52
